TPU v7x, 256 devices: a whole 4x4x8 slice. The times are simulated.
256 devices in a mesh: grp: 2 (over core), seq: 32 (over y, z), head: 4 (over x).
Axes of the slice: x: 4, y: 4, z: 8, core: 2. Of those that a mesh axis runs over, the one named last changes fastest.
Arguments:
- queries: bfloat16 [16384, 8192], P('seq', ('grp', 'head')), may hold values from -140 to 140
- key_rows: bfloat16 [16384, 1024], P('seq', ('grp', 'head')), may hold values from -6 to 6
- values: bfloat16 [16384, 1024], P('seq', ('grp', 'head')), may hold values from -6 to 6
- out_grad: bfloat16 [16384, 8192], P('seq', ('grp', 'head')), may hold values from -6 to 6
- teacher_window: bfloat16 [128, 3, 64, 128, 128], P('seq', None, ('grp', 'head')), may hold values from -16 to 250
- teacher_global: bfloat16 [128, 2, 64, 128, 128], P('seq', None, ('grp', 'head')), may hold values from -16 to 250
- global_picks: int32 [128, 2], P('seq'), may hold values from -1 to 3, as said below
- mix_weight: float32 [16384], P('seq'), may hold values from 0.05 to 0.95
Outputs:
- query_grad: bfloat16 [16384, 8192], P('seq', ('grp', 'head'))
- key_grad: bfloat16 [16384, 1024], P('seq', ('grp', 'head'))
- value_grad: bfloat16 [16384, 1024], P('seq', ('grp', 'head'))
- row_loss: float32 [16384], P('seq')
Inputs may be any that keep to these rules, and one draw needn't show every extreme that they name: `global_picks`: in each row the non-negative entries are distinct, and an entry of query block b is below b - 2.
All inputs are finite; a program needn't handle non-finite values.
Results may differ from a plain program's by a relative error of at most 0.005.
Values may be sent and summed in bfloat16 or wider, within the bound.
A program may use at most 128 MiB of HBM per device.

v0:
```python
import functools
import math

import jax
import jax.numpy as jnp
import numpy as np
from jax import lax
from jax.sharding import PartitionSpec as P

E = 128
BLK = 128
WIN = 3
NGLOB = 4


def passed_along(block, axis, distance):
    devices = range(lax.axis_size(axis))
    route = [(i - distance, i) for i in devices if i - distance in devices]
    return lax.ppermute(block, axis, route)


def split_up(x, dim, devices):
    before, after = (x.shape[:dim], x.shape[dim + 1 :])
    return jnp.moveaxis(x.reshape(*before, devices, -1, *after), dim, 0)


def sum_at_owner(x, axis, dim):
    devices = lax.axis_size(axis)
    blocks = lax.all_to_all(split_up(x, dim, devices), axis, 0, 0, tiled=True)
    return jnp.sum(blocks.astype(jnp.float32), axis=0)


def rows_for(lines, devices):
    spare = -lines.shape[0] % devices
    if not spare:
        return lines
    return jnp.concatenate([lines, jnp.zeros((spare, *lines.shape[1:]), lines.dtype)])


def in_order(blocks, dim):
    lengths = list(blocks.shape[1:])
    lengths[dim] *= blocks.shape[0]
    return jnp.moveaxis(blocks, 0, dim).reshape(lengths)


def sent_to_all(x, axis):
    copies = jnp.broadcast_to(x, (lax.axis_size(axis), *x.shape))
    return lax.all_to_all(copies, axis, split_axis=0, concat_axis=0, tiled=True)


def gather_directly(x, axis, dim):
    return in_order(sent_to_all(x, axis), dim)


def total_of(x, axes):
    lines = x.reshape(-1, x.shape[-1])
    own = sum_at_owner(rows_for(lines, lax.axis_size(axes)), axes, 0)
    whole = gather_directly(own.astype(jnp.bfloat16), axes, 0)
    return whole[: len(lines)].reshape(x.shape).astype(jnp.float32)


def sum_at_owner_2(x, axis, dim):
    blocks = split_up(x, dim, lax.axis_size(axis))
    arrived = lax.all_to_all(blocks, axis, split_axis=0, concat_axis=0, tiled=True)
    return arrived.sum(axis=0)


def taken_together(x, axis):
    return sent_to_all(x, axis).sum(axis=0)


def block_terms(
    query_tiles, key_cat, value_cat, teacher_cat, live_slots, grad_tiles, weights, scale
):
    nblk, rows, kv_heads, group, width = query_tiles.shape
    slots = key_cat.shape[1]
    scores = (
        jnp.einsum("bqnge,bsjne->bsngqj", query_tiles, key_cat, preferred_element_type=jnp.float32)
        * scale
    )
    causal = lax.broadcasted_iota(jnp.int32, (rows, rows), 1) <= lax.broadcasted_iota(
        jnp.int32, (rows, rows), 0
    )
    later_slot = jnp.arange(slots) > 0
    live = live_slots[:, :, None, None, None, None] & (
        causal[None, None, None, None] | later_slot[None, :, None, None, None, None]
    )
    masked = jnp.where(live, scores, -1000000000.0)
    shifted = masked - jnp.max(masked, axis=(1, 5), keepdims=True)
    expo = jnp.where(live, jnp.exp(shifted), 0.0)
    total = jnp.sum(expo, axis=(1, 5), keepdims=True)
    student_p = expo / total
    student_logp = shifted - jnp.log(total)
    teacher_grouped = teacher_cat.reshape(nblk, slots, kv_heads, group, rows, rows)
    teacher = jnp.where(live, teacher_grouped.astype(jnp.float32), -1000000000.0)
    teacher_shift = teacher - jnp.max(teacher, axis=(1, 5), keepdims=True)
    teacher_exp = jnp.where(live, jnp.exp(teacher_shift), 0.0)
    teacher_total = jnp.sum(teacher_exp, axis=(1, 5), keepdims=True)
    teacher_p = teacher_exp / teacher_total
    teacher_logp = teacher_shift - jnp.log(teacher_total)
    forward_kl = jnp.sum(
        jnp.where(live, teacher_p * (teacher_logp - student_logp), 0.0), axis=(1, 5), keepdims=True
    )
    reverse_kl = jnp.sum(
        jnp.where(live, student_p * (student_logp - teacher_logp), 0.0), axis=(1, 5), keepdims=True
    )
    mixing = weights[:, None, None, None, :, None]
    row_terms = jnp.sum(mixing * forward_kl + (1.0 - mixing) * reverse_kl, axis=(1, 2, 3, 5))
    probs_low = student_p.astype(jnp.bfloat16)
    prob_grad = jnp.einsum(
        "bqnge,bsjne->bsngqj", grad_tiles, value_cat, preferred_element_type=jnp.float32
    )
    delta = jnp.sum(student_p * prob_grad, axis=(1, 5), keepdims=True)
    score_grad = (
        jnp.where(
            live,
            mixing * (student_p - teacher_p)
            + (1.0 - mixing) * student_p * (student_logp - teacher_logp - reverse_kl)
            + student_p * (prob_grad - delta),
            0.0,
        )
        * scale
    )
    score_low = score_grad.astype(jnp.bfloat16)
    query_part = jnp.einsum(
        "bsngqj,bsjne->bqnge", score_low, key_cat, preferred_element_type=jnp.float32
    )
    key_part = jnp.einsum(
        "bsngqj,bqnge->bsjne", score_low, query_tiles, preferred_element_type=jnp.float32
    )
    value_part = jnp.einsum(
        "bsngqj,bqnge->bsjne", probs_low, grad_tiles, preferred_element_type=jnp.float32
    )
    return (query_part, key_part, value_part, row_terms)


def local(
    queries, key_rows, values, out_grad, teacher_window, teacher_global, global_picks, mix_weight
):
    tokens_here, columns = queries.shape
    key_columns = key_rows.shape[1]
    heads_here = teacher_window.shape[2]
    kv_here = key_columns // E
    group = heads_here // kv_here
    blocks_here = tokens_here // BLK
    lead = WIN - 1
    scale = 1.0 / math.sqrt(E)
    query_tiles = queries.reshape(blocks_here, BLK, kv_here, group, E)
    key_tiles = key_rows.reshape(blocks_here, BLK, kv_here, E)
    value_tiles = values.reshape(blocks_here, BLK, kv_here, E)
    grad_tiles = out_grad.reshape(blocks_here, BLK, kv_here, group, E)
    at_root = lax.axis_index("seq") == 0
    tail_pair = jnp.stack([key_tiles[blocks_here - lead :], value_tiles[blocks_here - lead :]])
    before = passed_along(tail_pair, "seq", 1)
    own_sinks = jnp.where(at_root, jnp.stack([key_tiles, value_tiles]).astype(jnp.float32), 0.0)
    sink_pair = total_of(own_sinks.astype(jnp.bfloat16), "seq").astype(jnp.bfloat16)
    crossing = [(q_block, offset) for offset in range(1, WIN) for q_block in range(offset)]
    outgoing = jnp.stack(
        [teacher_window[blocks_here + q_block - offset, offset] for q_block, offset in crossing]
    )
    incoming = passed_along(outgoing, "seq", 1)
    key_extended = jnp.concatenate([before[0], key_tiles], axis=0)
    value_extended = jnp.concatenate([before[1], value_tiles], axis=0)
    window_index = np.array(
        [[q_block + lead - offset for offset in range(WIN)] for q_block in range(blocks_here)],
        dtype=np.int32,
    )
    safe_picks = jnp.maximum(global_picks, 0)
    key_cat = jnp.concatenate(
        [key_extended[window_index], jnp.take(sink_pair[0], safe_picks, axis=0)], axis=1
    )
    value_cat = jnp.concatenate(
        [value_extended[window_index], jnp.take(sink_pair[1], safe_picks, axis=0)], axis=1
    )
    window_tiles = []
    for q_block in range(blocks_here):
        for offset in range(WIN):
            if q_block >= offset:
                window_tiles.append(teacher_window[q_block - offset, offset])
            else:
                window_tiles.append(incoming[crossing.index((q_block, offset))])
    teacher_cat = jnp.concatenate(
        [jnp.stack(window_tiles).reshape(blocks_here, WIN, heads_here, BLK, BLK), teacher_global],
        axis=1,
    )
    block_ids = lax.axis_index("seq") * blocks_here + jnp.arange(blocks_here, dtype=jnp.int32)
    live_window = block_ids[:, None] - jnp.arange(WIN, dtype=jnp.int32)[None, :] >= 0
    live_slots = jnp.concatenate([live_window, global_picks >= 0], axis=1)
    query_part, key_part, value_part, row_terms = block_terms(
        query_tiles,
        key_cat,
        value_cat,
        teacher_cat,
        live_slots,
        grad_tiles,
        mix_weight.reshape(blocks_here, BLK),
        scale,
    )
    key_lists = [[] for _ in range(blocks_here + lead)]
    value_lists = [[] for _ in range(blocks_here + lead)]
    for q_block in range(blocks_here):
        for offset in range(WIN):
            key_lists[q_block + lead - offset].append(key_part[q_block, offset])
            value_lists[q_block + lead - offset].append(value_part[q_block, offset])
    key_summed = jnp.stack([functools.reduce(jnp.add, entries) for entries in key_lists])
    value_summed = jnp.stack([functools.reduce(jnp.add, entries) for entries in value_lists])
    sink_terms = []
    for sink_id in range(NGLOB):
        chosen = (global_picks == sink_id)[:, :, None, None, None]
        sink_terms.append(
            jnp.stack(
                [
                    jnp.sum(jnp.where(chosen, key_part[:, WIN:], 0.0), axis=(0, 1)),
                    jnp.sum(jnp.where(chosen, value_part[:, WIN:], 0.0), axis=(0, 1)),
                ]
            )
        )
    sink_local = jnp.stack(sink_terms, axis=1)
    returned = passed_along(
        jnp.stack([key_summed[:lead], value_summed[:lead]]).astype(jnp.bfloat16), "seq", -1
    ).astype(jnp.float32)
    flat_terms = sink_local.reshape(2, NGLOB * BLK, kv_here * E)
    shares = sum_at_owner_2(flat_terms, "seq", 1)
    sink_total = gather_directly(shares, "seq", 1).reshape(sink_local.shape)
    key_own = key_summed[lead:].at[blocks_here - lead :].add(returned[0])
    value_own = value_summed[lead:].at[blocks_here - lead :].add(returned[1])
    key_own = key_own.at[:NGLOB].add(jnp.where(at_root, sink_total[0], 0.0))
    value_own = value_own.at[:NGLOB].add(jnp.where(at_root, sink_total[1], 0.0))
    row_loss = taken_together(row_terms, ("grp", "head")).reshape(tokens_here)
    query_grad = query_part.reshape(tokens_here, columns).astype(jnp.bfloat16)
    key_grad = key_own.reshape(tokens_here, key_columns).astype(jnp.bfloat16)
    value_grad = value_own.reshape(tokens_here, key_columns).astype(jnp.bfloat16)
    return (query_grad, key_grad, value_grad, row_loss)


def solution(mesh):
    placed = (
        P("seq", ("grp", "head")),
        P("seq", ("grp", "head")),
        P("seq", ("grp", "head")),
        P("seq", ("grp", "head")),
        P("seq", None, ("grp", "head"), None, None),
        P("seq", None, ("grp", "head"), None, None),
        P("seq", None),
        P("seq"),
    )
    return jax.shard_map(
        local,
        mesh=mesh,
        in_specs=placed,
        out_specs=(
            P("seq", ("grp", "head")),
            P("seq", ("grp", "head")),
            P("seq", ("grp", "head")),
            P("seq"),
        ),
        check_vma=False,
    )
```

profile of v0, /device:TPU:4, one launch (start us, length us, event | category | flops | bytes accessed | tf_op | source)
XLA Modules:
  0.0 185.5 jit_solution(15815412904630939797)
XLA Ops:
  2.9 4.8 %collective-permute-start.1 = (bf16[3,8,128,128]{3,2,1,0:T(8,128)(2,1)}, bf16[3,8,128,128]{3,2,1,0:T(8,128)(2,1)}, u32[]{:S(2)}, u32[]{:S(2)}) collective-permute-start(bf16[3,8,128,128]{3,2,1,0:T(8,128)(2,1)} %pad_maximum_fusion.1), channel_id=1, source_target_pairs={{0,4},{4,8},{8,12},{12,16},{16,20},{20,24},{24,28},{28,32},{32,36}... | collective-permute-start | bytes 2359304 | tf_op jit(solution)/shard_map/ppermute | solution.py:19
  9.4 9.8 %all-to-all-start = ((bf16[32,32,128]{2,1,0:T(8,128)(2,1)}), bf16[32,32,128]{2,1,0:T(8,128)(2,1)}, u32[]{:S(2)}, u32[]{:S(2)}) async-start(bf16[32,32,128]{2,1,0:T(8,128)(2,1)} %bitcast.8), calls=%async_computation | async-start | bytes 524288 | tf_op jit(solution)/shard_map/all_to_all | solution.py:29
  21.7 4.3 %collective-permute-start = (bf16[2,2,128,1,128]{4,2,1,3,0:T(8,128)(2,1)}, bf16[2,2,128,1,128]{4,2,1,3,0:T(8,128)(2,1)}, u32[]{:S(2)}, u32[]{:S(2)}) collective-permute-start(bf16[2,2,128,1,128]{4,2,1,3,0:T(8,128)(2,1)} %pad_maximum_fusion.8), channel_id=1, source_target_pairs={{0,4},{4,8},{8,12},{12,16},{16,20},{20,24},{24,28},{28,32},{32,36}... | collective-permute-start | bytes 393224 | tf_op jit(solution)/shard_map/ppermute | solution.py:19
  34.6 4.0 %copy.185 = bf16[4,2,8,128,128]{3,4,2,1,0:T(8,128)(2,1)} copy(bf16[4,2,8,128,128]{4,3,2,1,0:T(8,128)(2,1)} %param.30) | data formatting | bytes 4194304 | tf_op args[5]
  42.4 1.8 maximum_bitcast_fusion.2
  44.2 2.3 %gather_fusion = bf16[12,128,128]{2,1,0:T(8,128)(2,1)} fusion(bf16[6,128,128]{2,1,0:T(8,128)(2,1)} %get-tuple-element.118, s32[1024]{0:T(1024)S(1)} %get-tuple-element.117), kind=kCustom, calls=%fused_computation.2 | custom fusion | bytes 786480 | tf_op jit(solution)/shard_map/gather | solution.py:170
  46.5 2.3 %gather_fusion.1 = bf16[12,128,128]{2,1,0:T(8,128)(2,1)} fusion(bf16[6,128,128]{2,1,0:T(8,128)(2,1)} %get-tuple-element.119, s32[1024]{0:T(1024)S(1)} %get-tuple-element.117), kind=kCustom, calls=%fused_computation.3 | custom fusion | bytes 786480 | tf_op jit(solution)/shard_map/gather | solution.py:173
  50.5 8.2 %all-to-all-start.1 = ((bf16[32,32,128]{2,1,0:T(8,128)(2,1)}), bf16[32,32,128]{2,1,0:T(8,128)(2,1)}, u32[]{:S(2)}, u32[]{:S(2)}) async-start(bf16[32,32,128]{2,1,0:T(8,128)(2,1)} %broadcast_in_dim.135), calls=%async_computation.1 | async-start | bytes 524288 | tf_op jit(solution)/shard_map/all_to_all | solution.py:48
  58.7 1.9 %slice_dynamic-update-slice_fusion = bf16[12,8,128,128]{3,2,1,0:T(8,128)(2,1)} fusion(bf16[12,8,128,128]{3,2,1,0:T(8,128)(2,1)} %bitcast_dynamic-update-slice_fusion.8, bf16[3,8,128,128]{3,2,1,0:T(8,128)(2,1)} %collective-permute-done.1), kind=kLoop, calls=%fused_computation.55 | loop fusion | bytes 1048576
  68.1 3.5 %copy.184 = bf16[12,8,128,128]{2,3,1,0:T(8,128)(2,1)S(1)} copy(bf16[12,8,128,128]{3,2,1,0:T(8,128)(2,1)} %bitcast_dynamic-update-slice_fusion) | data formatting | bytes 6291456 | tf_op jit(solution)/shard_map/stack | solution.py:183
  73.3 2.2 %gather_fusion.2 = bf16[8,128,128]{2,1,0:T(8,128)(2,1)} fusion(bf16[4,128,128]{2,1,0:T(8,128)(2,1)} %bitcast.295, s32[1024]{0:T(1024)S(1)} %get-tuple-element.116), kind=kCustom, calls=%fused_computation.clone | custom fusion | bytes 524320 | tf_op jit(solution)/shard_map/jit(_take)/gather | solution.py:170
  75.5 2.2 %gather_fusion.3 = bf16[8,128,128]{2,1,0:T(8,128)(2,1)} fusion(bf16[4,128,128]{2,1,0:T(8,128)(2,1)} %bitcast.294, s32[1024]{0:T(1024)S(1)} %get-tuple-element.116), kind=kCustom, calls=%fused_computation.1.clone | custom fusion | bytes 524320 | tf_op jit(solution)/shard_map/jit(_take)/gather | solution.py:173
  79.5 5.0 %fusion.7 = (f32[4,8,128]{2,1,0:T(8,128)S(1)}, f32[4,8,128]{2,1,0:T(8,128)S(1)}, f32[4,5,128,128,8]{3,2,4,1,0:T(8,128)S(1)}) fusion(pred[4,5,128,128]{2,3,1,0:T(8,128)(4,1)S(1)} %broadcast_and_fusion, bf16[4,2,1,8,128,128]{4,5,3,1,0,2:T(8,128)(2,1)} %bitcast.276, bf16[4,3,1,8,128,128]{4,5,3,1,0,2:T(8,128)(2,1)S(1)} %bitcast.272, ...), kind=kOutput, calls=%fused_computation.18 | convolution fusion | flops 690741248 | bytes 17793024 | tf_op jit(solution)/shard_map/bqnge,bsjne->bsngqj/dot_general | solution.py:78
  84.6 5.0 %fusion.11 = (f32[4,8,128]{2,1,0:T(8,128)S(1)}, f32[4,8,128]{2,1,0:T(8,128)S(1)}) fusion(f32[4,8,128]{2,1,0:T(8,128)S(1)} %get-tuple-element.82, pred[4,5,128,128]{2,3,1,0:T(8,128)(4,1)S(1)} %broadcast_and_fusion, bf16[4,2,1,8,128,128]{4,5,3,1,0,2:T(8,128)(2,1)S(1)} %bitcast.278, bf16[4,3,1,8,128,128]{4,5,3,1,0,2:T(8,128)(2,1)S(1)} %bitcast.273, ...), kind=kLoop, calls=%fused_computation.22 | loop fusion | flops 28827648 | bytes 16121856 | tf_op jit(solution)/shard_map/reduce_sum | solution.py:98
  89.6 3.5 %fusion.16 = f32[4,5,128,128,1]{3,2,4,1,0:T(8,128)S(1)} fusion(bf16[4,128,8,128,1]{3,2,1,0,4:T(8,128)(2,1)S(1)} %copy-done.6, f32[4,8,128]{2,1,0:T(8,128)S(1)} %get-tuple-element.81, pred[4,5,128,128]{2,3,1,0:T(8,128)(4,1)S(1)} %broadcast_and_fusion, f32[4,8,128]{2,1,0:T(8,128)S(1)} %get-tuple-element.83, f32[4,5,128,128,8]{3,2,4,1,0:T(8,128)S(1)} %get-tuple-element.114), kind=kOutput, calls=%fused_computation.29 | convolution fusion | flops 686817280 | bytes 13205504 | tf_op jit(solution)/shard_map/bsngqj,bqnge->bsjne/dot_general | solution.py:131
  94.9 12.0 %select_reduce_fusion = (f32[4,8,128]{2,1,0:T(8,128)}, f32[4,8,128]{2,1,0:T(8,128)S(1)}, f32[4,8,128]{2,1,0:T(8,128)S(1)}, f32[4,5,128,128,8]{3,2,4,1,0:T(8,128)}) fusion(f32[4,8,128]{2,1,0:T(8,128)S(1)} %log.17, f32[4,8,128]{2,1,0:T(8,128)S(1)} %log.16, f32[4,8,128]{2,1,0:T(8,128)S(1)} %get-tuple-element.80, f32[4,8,128]{2,1,0:T(8,128)S(1)} %get-tuple-element.82, ...), kind=kOutput, calls=%fused_computation.13 | convolution fusion | flops 732680192 | bytes 28393472 | tf_op jit(solution)/shard_map/bqnge,bsjne->bsngqj/dot_general | solution.py:110
  106.9 12.1 %fusion.5 = bf16[4,5,1,8,128,128]{4,5,3,1,0,2:T(8,128)(2,1)S(1)} fusion(f32[4,5,128,128,8]{3,2,4,1,0:T(8,128)} %get-tuple-element.115, f32[4,8,128]{2,1,0:T(8,128)S(1)} %get-tuple-element.71, f32[4,8,128]{2,1,0:T(8,128)S(1)} %get-tuple-element.70, f32[4,8,128]{2,1,0:T(8,128)S(1)} %log.17, f32[4,8,128]{2,1,0:T(8,128)S(1)} %log.16, ...), kind=kLoop, calls=%fused_computation.12 | loop fusion | flops 68157440 | bytes 31920128 | tf_op jit(solution)/shard_map/convert_element_type | solution.py:124
  119.0 2.3 %copy-done = bf16[4,5,1,8,128,128]{4,5,3,1,0,2:T(8,128)(2,1)} copy-done((bf16[4,5,1,8,128,128]{4,5,3,1,0,2:T(8,128)(2,1)}, bf16[4,5,1,8,128,128]{4,5,3,1,0,2:T(8,128)(2,1)S(1)}, u32[]{:S(2)}) %copy-start) | copy-done | bytes 5242904
  125.5 9.5 %all-to-all-start.2 = ((f32[32,2,16,128]{3,2,1,0:T(8,128)}), f32[32,2,16,128]{3,2,1,0:T(8,128)S(1)}, u32[]{:S(2)}, u32[]{:S(2)}) async-start(f32[32,2,16,128]{3,2,1,0:T(8,128)} %copy.213), calls=%async_computation.2 | async-start | bytes 1048576 | tf_op jit(solution)/shard_map/all_to_all | solution.py:64
  136.0 14.0 %all-to-all-done.2 = f32[32,2,16,128]{3,2,1,0:T(8,128)S(1)} async-done(((f32[32,2,16,128]{3,2,1,0:T(8,128)}), f32[32,2,16,128]{3,2,1,0:T(8,128)S(1)}, u32[]{:S(2)}, u32[]{:S(2)}) %all-to-all-start.2) | async-done | bytes 524320 | tf_op jit(solution)/shard_map/all_to_all | solution.py:64
  150.6 4.8 %all-to-all-start.4 = ((f32[8,4,128]{2,1,0:T(4,128)}), f32[8,4,128]{2,1,0:T(4,128)S(1)}, u32[]{:S(2)}, u32[]{:S(2)}) async-start(f32[8,4,128]{2,1,0:T(4,128)} %broadcast_in_dim.147), calls=%async_computation.4 | async-start | bytes 32768 | tf_op jit(solution)/shard_map/all_to_all | solution.py:48
  159.2 8.2 %all-to-all-start.3 = ((f32[32,2,16,128]{3,2,1,0:T(8,128)}), f32[32,2,16,128]{3,2,1,0:T(8,128)S(1)}, u32[]{:S(2)}, u32[]{:S(2)}) async-start(f32[32,2,16,128]{3,2,1,0:T(8,128)} %broadcast_in_dim.145), calls=%async_computation.3 | async-start | bytes 1048576 | tf_op jit(solution)/shard_map/all_to_all | solution.py:48
  167.4 3.5 %fusion.25 = bf16[4,128,1,8,128]{1,4,3,0,2:T(8,128)(2,1)S(1)} fusion(bf16[4,5,1,8,128,128]{4,5,3,1,0,2:T(8,128)(2,1)} %copy-done, bf16[4,2,128,1,128]{4,2,1,0,3:T(8,128)(2,1)S(1)} %copy-done.8, bf16[4,3,128,1,128]{4,2,1,0,3:T(8,128)(2,1)S(1)} %bitcast.289), kind=kOutput, calls=%fused_computation.37 | convolution fusion | flops 672923648 | bytes 6946816 | tf_op jit(solution)/shard_map/bsngqj,bsjne->bqnge/dot_general | solution.py:125
  174.5 9.6 %all-to-all-done.3 = f32[32,2,16,128]{3,2,1,0:T(8,128)S(1)} async-done(((f32[32,2,16,128]{3,2,1,0:T(8,128)}), f32[32,2,16,128]{3,2,1,0:T(8,128)S(1)}, u32[]{:S(2)}, u32[]{:S(2)}) %all-to-all-start.3) | async-done | bytes 524320 | tf_op jit(solution)/shard_map/all_to_all | solution.py:48
  (131 shorter events, 47.6 us)
Async XLA Ops:
  0.6 40.8 %copy-start.23 = (s32[12]{0:T(128)S(1)}, s32[12]{0:T(128)}, u32[]{:S(2)}) copy-start(s32[12]{0:T(128)} %constant.166) | copy-start | bytes 148
  0.6 33.9 %copy-start.18 = (s32[4,2]{0,1:T(2,128)S(1)}, s32[4,2]{0,1:T(2,128)}, u32[]{:S(2)}) copy-start(s32[4,2]{0,1:T(2,128)} %param.31) | copy-start | bytes 100
  0.7 33.3 %copy-start.12 = (f32[512]{0:T(512)S(1)}, f32[512]{0:T(512)}, u32[]{:S(2)}) copy-start(f32[512]{0:T(512)} %param.32) | copy-start | bytes 6148
  1.9 58.8 %copy-start.3 = (bf16[4,3,8,128,128]{4,3,2,1,0:T(8,128)(2,1)S(1)}, bf16[4,3,8,128,128]{4,3,2,1,0:T(8,128)(2,1)}, u32[]{:S(2)}) copy-start(bf16[4,3,8,128,128]{4,3,2,1,0:T(8,128)(2,1)} %param.29) | copy-start | bytes 9437188
  2.9 55.9 %collective-permute-start.1 = (bf16[3,8,128,128]{3,2,1,0:T(8,128)(2,1)}, bf16[3,8,128,128]{3,2,1,0:T(8,128)(2,1)}, u32[]{:S(2)}, u32[]{:S(2)}) collective-permute-start(bf16[3,8,128,128]{3,2,1,0:T(8,128)(2,1)} %pad_maximum_fusion.1), channel_id=1, source_target_pairs={{0,4},{4,8},{8,12},{12,16},{16,20},{20,24},{24,28},{28,32},{32,36}... | collective-permute-start | bytes 2359304 | tf_op jit(solution)/shard_map/ppermute | solution.py:19
  9.4 39.3 %all-to-all-start = ((bf16[32,32,128]{2,1,0:T(8,128)(2,1)}), bf16[32,32,128]{2,1,0:T(8,128)(2,1)}, u32[]{:S(2)}, u32[]{:S(2)}) async-start(bf16[32,32,128]{2,1,0:T(8,128)(2,1)} %bitcast.8), calls=%async_computation | async-start | bytes 524288 | tf_op jit(solution)/shard_map/all_to_all | solution.py:29
  21.7 19.8 %collective-permute-start = (bf16[2,2,128,1,128]{4,2,1,3,0:T(8,128)(2,1)}, bf16[2,2,128,1,128]{4,2,1,3,0:T(8,128)(2,1)}, u32[]{:S(2)}, u32[]{:S(2)}) collective-permute-start(bf16[2,2,128,1,128]{4,2,1,3,0:T(8,128)(2,1)} %pad_maximum_fusion.8), channel_id=1, source_target_pairs={{0,4},{4,8},{8,12},{12,16},{16,20},{20,24},{24,28},{28,32},{32,36}... | collective-permute-start | bytes 393224 | tf_op jit(solution)/shard_map/ppermute | solution.py:19
  50.5 21.1 %all-to-all-start.1 = ((bf16[32,32,128]{2,1,0:T(8,128)(2,1)}), bf16[32,32,128]{2,1,0:T(8,128)(2,1)}, u32[]{:S(2)}, u32[]{:S(2)}) async-start(bf16[32,32,128]{2,1,0:T(8,128)(2,1)} %broadcast_in_dim.135), calls=%async_computation.1 | async-start | bytes 524288 | tf_op jit(solution)/shard_map/all_to_all | solution.py:48
  106.9 14.4 %copy-start.2 = (bf16[4,128,8,128,1]{3,2,1,0,4:T(8,128)(2,1)S(1)}, bf16[4,128,8,128,1]{3,2,1,0,4:T(8,128)(2,1)}, u32[]{:S(2)}) copy-start(bf16[4,128,8,128,1]{3,2,1,0,4:T(8,128)(2,1)} %bitcast_bitcast_fusion.1) | copy-start | bytes 3145732
  106.9 16.0 %copy-start.19 = (pred[4,2]{1,0:T(4,128)(4,1)S(1)}, pred[4,2]{1,0:T(4,128)(4,1)}, u32[]{:S(2)}) copy-start(pred[4,2]{1,0:T(4,128)(4,1)} %copy.209) | copy-start | bytes 28
  106.9 16.0 %copy-start.20 = (pred[4,2]{1,0:T(4,128)(4,1)S(1)}, pred[4,2]{1,0:T(4,128)(4,1)}, u32[]{:S(2)}) copy-start(pred[4,2]{1,0:T(4,128)(4,1)} %copy.210) | copy-start | bytes 28
  106.9 16.0 %copy-start.21 = (pred[4,2]{1,0:T(4,128)(4,1)S(1)}, pred[4,2]{1,0:T(4,128)(4,1)}, u32[]{:S(2)}) copy-start(pred[4,2]{1,0:T(4,128)(4,1)} %copy.211) | copy-start | bytes 28
  106.9 16.0 %copy-start.22 = (pred[4,2]{1,0:T(4,128)(4,1)S(1)}, pred[4,2]{1,0:T(4,128)(4,1)}, u32[]{:S(2)}) copy-start(pred[4,2]{1,0:T(4,128)(4,1)} %copy.212) | copy-start | bytes 28
  121.3 13.7 %copy-start.14 = (f32[512]{0:T(512)S(1)}, f32[512]{0:T(512)}, u32[]{:S(2)}) copy-start(f32[512]{0:T(512)} %param.32) | copy-start | bytes 6148
  121.3 13.7 %copy-start.16 = (f32[4,128]{1,0:T(4,128)S(1)}, f32[4,128]{1,0:T(4,128)}, u32[]{:S(2)}) copy-start(f32[4,128]{1,0:T(4,128)} %broadcast_subtract_fusion) | copy-start | bytes 6148
  121.3 13.7 %copy-start.17 = (f32[4,8,128]{2,1,0:T(8,128)S(1)}, f32[4,8,128]{2,1,0:T(8,128)}, u32[]{:S(2)}) copy-start(f32[4,8,128]{2,1,0:T(8,128)} %get-tuple-element.69) | copy-start | bytes 49156
  121.4 13.7 %copy-start.10 = (bf16[1,128,1,128]{3,1,0,2:T(8,128)(2,1)S(1)}, bf16[1,128,1,128]{3,1,0,2:T(8,128)(2,1)}, u32[]{:S(2)}) copy-start(bf16[1,128,1,128]{3,1,0,2:T(8,128)(2,1)} %get-tuple-element.94) | copy-start | bytes 98308
  121.4 13.7 %copy-start.11 = (bf16[1,128,1,128]{3,1,0,2:T(8,128)(2,1)S(1)}, bf16[1,128,1,128]{3,1,0,2:T(8,128)(2,1)}, u32[]{:S(2)}) copy-start(bf16[1,128,1,128]{3,1,0,2:T(8,128)(2,1)} %fusion.53) | copy-start | bytes 98308
  121.4 46.0 %copy-start.4 = (bf16[12,128,128]{2,1,0:T(8,128)(2,1)S(1)}, bf16[12,128,128]{2,1,0:T(8,128)(2,1)}, u32[]{:S(2)}) copy-start(bf16[12,128,128]{2,1,0:T(8,128)(2,1)} %gather_fusion) | copy-start | bytes 1179652
  121.4 46.0 %copy-start.8 = (bf16[4,2,128,1,128]{4,2,1,0,3:T(8,128)(2,1)S(1)}, bf16[4,2,128,1,128]{4,2,1,0,3:T(8,128)(2,1)}, u32[]{:S(2)}) copy-start(bf16[4,2,128,1,128]{4,2,1,0,3:T(8,128)(2,1)} %copy-done.7) | copy-start | bytes 786436
  125.5 24.6 %all-to-all-start.2 = ((f32[32,2,16,128]{3,2,1,0:T(8,128)}), f32[32,2,16,128]{3,2,1,0:T(8,128)S(1)}, u32[]{:S(2)}, u32[]{:S(2)}) async-start(f32[32,2,16,128]{3,2,1,0:T(8,128)} %copy.213), calls=%async_computation.2 | async-start | bytes 1048576 | tf_op jit(solution)/shard_map/all_to_all | solution.py:64
  150.6 7.7 %all-to-all-start.4 = ((f32[8,4,128]{2,1,0:T(4,128)}), f32[8,4,128]{2,1,0:T(4,128)S(1)}, u32[]{:S(2)}, u32[]{:S(2)}) async-start(f32[8,4,128]{2,1,0:T(4,128)} %broadcast_in_dim.147), calls=%async_computation.4 | async-start | bytes 32768 | tf_op jit(solution)/shard_map/all_to_all | solution.py:48
  156.1 18.4 %collective-permute-start.2 = (bf16[2,2,128,1,128]{4,2,1,3,0:T(8,128)(2,1)}, bf16[2,2,128,1,128]{4,2,1,3,0:T(8,128)(2,1)S(1)}, u32[]{:S(2)}, u32[]{:S(2)}) collective-permute-start(bf16[2,2,128,1,128]{4,2,1,3,0:T(8,128)(2,1)} %pad_maximum_fusion.9), channel_id=1, source_target_pairs={{4,0},{8,4},{12,8},{16,12},{20,16},{24,20},{28,24},{32,28},{36,32}... | collective-permute-start | bytes 393224 | tf_op jit(solution)/shard_map/ppermute | solution.py:19
  159.2 24.9 %all-to-all-start.3 = ((f32[32,2,16,128]{3,2,1,0:T(8,128)}), f32[32,2,16,128]{3,2,1,0:T(8,128)S(1)}, u32[]{:S(2)}, u32[]{:S(2)}) async-start(f32[32,2,16,128]{3,2,1,0:T(8,128)} %broadcast_in_dim.145), calls=%async_computation.3 | async-start | bytes 1048576 | tf_op jit(solution)/shard_map/all_to_all | solution.py:48
  (8 other events, 43.6 us)
where the time goes:
time: 188 us; the launch traced here: 186 us
  local copies, waits for them, and re-layouts  51 us (27%)
  starting transfers between devices  51 us (27%)
  other arithmetic  32.3 us (17%)
  matrix products  25.5 us (14%)
  waiting for transfers between devices  24.5 us (13%)
    unnamed x62, local copies, waits for them, and re-layouts  22 us
    all_to_all x3, starting transfers between devices, sent_to_all(): return lax.all_to_all(copies, axis, split_axis=0, concat_axis=0, tiled=True)  21.2 us
    all_to_all x1, waiting for transfers between devices, sum_at_owner_2(): lax.all_to_all(blocks, axis, split_axis=0, concat_axis=0, tiled=True)  14 us
    convert_element_type x1, other arithmetic, block_terms(): score_low = score_grad.astype(jnp.bfloat16)  12.1 us
    dot_general x1, matrix products, block_terms(): jnp.einsum('bqnge,bsjne->bsngqj', grad_tiles, value_cat, preferred_elemen...  12 us
    all_to_all x3, waiting for transfers between devices, sent_to_all(): return lax.all_to_all(copies, axis, split_axis=0, concat_axis=0, tiled=True)  10.5 us
    ppermute x3, starting transfers between devices, passed_along(): return lax.ppermute(block, axis, route)  10.4 us
    all_to_all x1, starting transfers between devices, sum_at_owner(): blocks = lax.all_to_all(split_up(x, dim, devices), axis, 0, 0, tiled=True)  9.85 us
  transfers between devices with their start and end apart: 8, of which 3 were waited for; matrix products, arithmetic and copies ran while one was open for 28% of the time, Pallas kernels for 0%

commit v1 on v0

v1 whole, which is shorter than its diff:
```python
import functools
import math

import jax
import jax.numpy as jnp
from jax import lax
from jax.experimental import pallas as pl
from jax.experimental.pallas import tpu as pltpu
from jax.sharding import PartitionSpec as P

E = 128
BLK = 128
WIN = 3
NGLOB = 4
NB = 4
HEADS = 8
SLOTS = 5
ROWS = 16
LOG2E = math.log2(math.e)
LN2 = math.log(2.0)
SCALE = 1.0 / math.sqrt(E)
NEG = -1.0e30
MESH = pl.DeviceIdType.MESH
F32 = jnp.float32
BF16 = jnp.bfloat16
CHUNKS = 2 * NGLOB
LOCAL_TILES = [(c, d) for c in range(NB) for d in range(WIN) if c + d < NB]
CROSS = [(3, 2), (3, 1), (2, 2)]


def split_of(size):
    z = 1
    while size % z or size // z > z:
        z += 1
    return size // z, z


def kernel(
    nseq, ngrp, nhead,
    q_h, k_h, v_h, do_h, tw_h, tg_h, picks, mix_ref,
    qg_h, kgrad, vgrad, loss_out,
    q_v, do_v, tw_v, tg_v, th_v, k_v, v_v, glob, kc, vc,
    s_scr, dp_scr, sg_scr, p_scr, dkt, dvt, mixc, loss_scr, lbuf,
    acc_k, acc_v, sink, qg_v, sbuf, rbuf, hs, hr,
    lsem, hsend, hrecv, bsend, brecv, rsend, rrecv, gsend, grecv, lsend, lrecv, osem,
):
    ny, nz = split_of(nseq)
    seq = lax.axis_index("seq")
    grp = lax.axis_index("grp")
    head = lax.axis_index("head")
    y = seq // nz
    z = seq % nz
    zhalf, yhalf = nz // 2, ny // 2
    z_up, z_dn = lax.rem(z + 1, nz), lax.rem(z + nz - 1, nz)
    y_up, y_dn = lax.rem(y + 1, ny), lax.rem(y + ny - 1, ny)
    dev_zu, dev_zd = y * nz + z_up, y * nz + z_dn
    dev_yu, dev_yd = y_up * nz + z, y_dn * nz + z
    nxt, prv = lax.rem(seq + 1, nseq), lax.rem(seq + nseq - 1, nseq)
    kid_zu = (z < zhalf) if nz > 1 else (z < 0)
    kid_zd = ((z == 0) | (z > zhalf + 1)) if nz > 2 else (z < 0)
    kid_yu = (y < yhalf) if ny > 1 else (y < 0)
    kid_yd = ((y == 0) | (y > yhalf + 1)) if ny > 2 else (y < 0)
    kids = [
        [(0, dev_zu, kid_zu), (1, dev_zd, kid_zd), (2, dev_yu, kid_yu & (z == 0)), (3, dev_yd, kid_yd & (z == 0))],
        [(0, dev_zu, kid_zu & (y == 0)), (1, dev_zd, kid_zd & (y == 0)), (2, dev_yu, kid_yu), (3, dev_yd, kid_yd)],
    ]
    z_low = z <= zhalf
    y_low = y <= yhalf
    z_par = jnp.where(z_low, dev_zd, dev_zu)
    z_slot = jnp.where(z_low, 0, 1)
    y_par = jnp.where(y_low, dev_yd, dev_yu)
    y_slot = jnp.where(y_low, 2, 3)
    parents = [
        (jnp.where(z > 0, z_par, y_par), jnp.where(z > 0, z_slot, y_slot)),
        (jnp.where(y > 0, y_par, z_par), jnp.where(y > 0, y_slot, z_slot)),
    ]
    is_root = seq == 0

    loads = {}
    count = [0]

    def load(key, src, dst):
        copy = pltpu.make_async_copy(src, dst, lsem.at[count[0]])
        count[0] += 1
        copy.start()
        loads.setdefault(key, []).append(copy)

    load("kv", k_h, k_v.at[pl.ds(WIN - 1, NB)])
    load("kv", v_h, v_v.at[pl.ds(WIN - 1, NB)])
    for b in reversed(range(NB)):
        load(b, q_h.at[b], q_v.at[b])
        load(b, do_h.at[b], do_v.at[b])
        for c, d in LOCAL_TILES:
            if c + d == b:
                load(b, tw_h.at[c, d], tw_v.at[c, d])
        load(b, tg_h.at[b], tg_v.at[b])

    barrier = pltpu.get_barrier_semaphore()
    waits = 0
    for dev in (dev_zu, dev_zd, dev_yu, dev_yd, nxt, prv):
        pl.semaphore_signal(barrier, inc=1, device_id={"seq": dev}, device_id_type=MESH)
        waits += 1
    peers = []
    for off in range(1, ngrp * nhead):
        flat = lax.rem(grp * nhead + head + off, ngrp * nhead)
        peers.append((flat // nhead, flat % nhead))
    for pg, ph in peers:
        pl.semaphore_signal(barrier, inc=1, device_id={"grp": pg, "head": ph}, device_id_type=MESH)
        waits += 1
    pl.semaphore_wait(barrier, waits)

    def halo_copies():
        out = []
        ends = [
            (k_h.at[pl.ds(NB - WIN + 1, WIN - 1)], k_v.at[pl.ds(0, WIN - 1)]),
            (v_h.at[pl.ds(NB - WIN + 1, WIN - 1)], v_v.at[pl.ds(0, WIN - 1)]),
        ] + [(tw_h.at[c, d], th_v.at[i]) for i, (c, d) in enumerate(CROSS)]
        for i, (src, dst) in enumerate(ends):
            out.append(
                pltpu.make_async_remote_copy(
                    src, dst, hsend.at[i], hrecv.at[i], device_id={"seq": nxt}, device_id_type=MESH
                )
            )
        return out

    halo = halo_copies()

    @pl.when(seq < nseq - 1)
    def _():
        for copy in halo:
            copy.start()

    def bcast(c, slot, dev):
        return pltpu.make_async_remote_copy(
            glob.at[c], glob.at[c], bsend.at[slot, c], brecv.at[c],
            device_id={"seq": dev}, device_id_type=MESH,
        )

    @pl.when(is_root)
    def _():
        a = pltpu.make_async_copy(k_h, glob.at[pl.ds(0, NGLOB)], lsem.at[count[0]])
        b = pltpu.make_async_copy(v_h, glob.at[pl.ds(NGLOB, NGLOB)], lsem.at[count[0] + 1])
        a.start()
        b.start()
        k_v[pl.ds(0, WIN - 1)] = jnp.zeros((WIN - 1, BLK, E), BF16)
        v_v[pl.ds(0, WIN - 1)] = jnp.zeros((WIN - 1, BLK, E), BF16)
        th_v[...] = jnp.zeros_like(th_v)
        a.wait()
        b.wait()

    order = [0, 2, 1, 3, 4, 6, 5, 7]
    for c in order:
        tree = (c // 2) % 2

        @pl.when(jnp.logical_not(is_root))
        def _():
            bcast(c, 0, parents[tree][0]).wait_recv()

        for slot, dev, cond in kids[tree]:

            @pl.when(cond)
            def _():
                bcast(c, slot, dev).start()

    for b in range(NB):
        mixc[b] = jnp.broadcast_to(mix_ref[pl.ds(b, 1), :], (BLK, BLK)).T
    acc_k[...] = jnp.zeros_like(acc_k)
    acc_v[...] = jnp.zeros_like(acc_v)
    sink[...] = jnp.zeros_like(sink)

    for copy in loads["kv"]:
        copy.wait()

    col = lax.broadcasted_iota(jnp.int32, (ROWS, BLK), 1)
    row = lax.broadcasted_iota(jnp.int32, (ROWS, BLK), 0)
    dims_t = (((1,), (1,)), ((), ()))
    dims_c = (((0,), (0,)), ((), ()))

    def halo_wait(indices):
        @pl.when(seq > 0)
        def _():
            for i in indices:
                halo[i].wait_recv()

    def block(b):
        if b == 1:
            halo_wait([0, 1, 2])
        if b == 0:
            halo_wait([3, 4])
        for copy in loads[b]:
            copy.wait()
        for d in range(WIN):
            kc[pl.ds(d * BLK, BLK), :] = k_v[b + WIN - 1 - d]
            vc[pl.ds(d * BLK, BLK), :] = v_v[b + WIN - 1 - d]
        biases = [None] * SLOTS
        for d in range(1, WIN):
            if b < d:
                biases[d] = jnp.where(seq > 0, 0.0, NEG)
        for g in range(SLOTS - WIN):
            pick = picks[b, g]
            safe = jnp.maximum(pick, 0)
            kc[pl.ds((WIN + g) * BLK, BLK), :] = glob[safe]
            vc[pl.ds((WIN + g) * BLK, BLK), :] = glob[safe + NGLOB]
            biases[WIN + g] = jnp.where(pick >= 0, 0.0, NEG)
        tiles = []
        for d in range(WIN):
            if b >= d:
                tiles.append(tw_v.at[b - d, d])
            else:
                tiles.append(th_v.at[CROSS.index((NB + b - d, d))])
        for g in range(SLOTS - WIN):
            tiles.append(tg_v.at[b, g])
        dkt[...] = jnp.zeros_like(dkt)
        dvt[...] = jnp.zeros_like(dvt)
        loss_scr[...] = jnp.zeros_like(loss_scr)

        def pair(i, carry):
            h0 = 2 * i
            lanes = [pl.ds(pl.multiple_of((h0 + e) * E, E), E) for e in range(2)]
            q2 = jnp.concatenate([q_v[b, :, lanes[0]], q_v[b, :, lanes[1]]], axis=0)
            do2 = jnp.concatenate([do_v[b, :, lanes[0]], do_v[b, :, lanes[1]]], axis=0)
            keys = kc[...]
            s_scr[...] = lax.dot_general(q2, keys, dims_t, preferred_element_type=F32)
            dp_scr[...] = lax.dot_general(do2, vc[...], dims_t, preferred_element_type=F32)
            for n in range(2 * BLK // ROWS):
                e, r0 = n // (BLK // ROWS), (n % (BLK // ROWS)) * ROWS
                at = pl.ds(n * ROWS, ROWS)
                ss, ts = [], []
                for j in range(SLOTS):
                    s = s_scr[at, pl.ds(j * BLK, BLK)] * (SCALE * LOG2E)
                    t = tiles[j][h0 + e, pl.ds(r0, ROWS), :].astype(F32) * LOG2E
                    if j == 0:
                        live = col <= row + r0
                        s = jnp.where(live, s, NEG)
                        t = jnp.where(live, t, NEG)
                    elif biases[j] is not None:
                        s = s + biases[j]
                        t = t + biases[j]
                    ss.append(s)
                    ts.append(t)
                m_s = jnp.max(functools.reduce(jnp.maximum, ss), axis=1, keepdims=True)
                m_t = jnp.max(functools.reduce(jnp.maximum, ts), axis=1, keepdims=True)
                mix = mixc[b, pl.ds(r0, ROWS), :]
                other = (1.0 - mix) * LN2
                es, et, xs = [], [], []
                z_s = z_t = f_u = r_u = x_u = None
                for j in range(SLOTS):
                    sp = ss[j] - m_s
                    tp = ts[j] - m_t
                    e_s = jnp.exp2(sp)
                    e_t = jnp.exp2(tp)
                    u = sp - tp
                    x = other * u + dp_scr[at, pl.ds(j * BLK, BLK)]
                    terms = (e_s, e_t, e_t * u, e_s * u, e_s * x)
                    if j == 0:
                        z_s, z_t, f_u, r_u, x_u = terms
                    else:
                        z_s, z_t, f_u, r_u, x_u = (
                            z_s + terms[0], z_t + terms[1], f_u + terms[2], r_u + terms[3], x_u + terms[4],
                        )
                    es.append(e_s)
                    et.append(e_t)
                    xs.append(x)
                z_s, z_t, f_u, r_u, x_u = (
                    jnp.sum(v, axis=1, keepdims=True) for v in (z_s, z_t, f_u, r_u, x_u)
                )
                i_s = 1.0 / z_s
                i_t = 1.0 / z_t
                c = jnp.log(z_t) - jnp.log(z_s)
                fkl = -(f_u * i_t * LN2 + c)
                rkl = r_u * i_s * LN2 + c
                loss_scr[pl.ds(r0, ROWS), :] += mix * fkl + (1.0 - mix) * rkl
                shift = mix - x_u * i_s
                t_fac = mix * i_t
                for j in range(SLOTS):
                    p = es[j] * i_s
                    p_scr[at, pl.ds(j * BLK, BLK)] = p.astype(BF16)
                    sg_scr[at, pl.ds(j * BLK, BLK)] = (p * (xs[j] + shift) - t_fac * et[j]).astype(BF16)
            sg = sg_scr[...]
            qg = (jnp.dot(sg, keys, preferred_element_type=F32) * SCALE).astype(BF16)
            qg_v[b, :, lanes[0]] = qg[:BLK]
            qg_v[b, :, lanes[1]] = qg[BLK:]
            dkt[...] += lax.dot_general(q2, sg, dims_c, preferred_element_type=F32)
            dvt[...] += lax.dot_general(do2, p_scr[...], dims_c, preferred_element_type=F32)
            return carry

        lax.fori_loop(0, HEADS // 2, pair, 0)
        pltpu.make_async_copy(qg_v.at[b], qg_h.at[b], osem.at[b]).start()
        for d in range(WIN):
            acc_k[b + WIN - 1 - d] += dkt[:, pl.ds(d * BLK, BLK)] * SCALE
            acc_v[b + WIN - 1 - d] += dvt[:, pl.ds(d * BLK, BLK)]
        for g in range(SLOTS - WIN):
            pick = picks[b, g]
            for n in range(NGLOB):
                hit = jnp.where(pick == n, 1.0, 0.0)
                sink[n] += dkt[:, pl.ds((WIN + g) * BLK, BLK)] * (hit * SCALE)
                sink[NGLOB + n] += dvt[:, pl.ds((WIN + g) * BLK, BLK)] * hit
        lbuf[0, pl.ds(b, 1), :] = loss_scr[...].T[0:1, :]

    for b in reversed(range(NB)):
        block(b)

    hs[0] = acc_k[pl.ds(0, WIN - 1)].astype(BF16)
    hs[1] = acc_v[pl.ds(0, WIN - 1)].astype(BF16)
    back = pltpu.make_async_remote_copy(
        hs, hr, gsend.at[0], grecv.at[0], device_id={"seq": prv}, device_id_type=MESH
    )

    loss_copies = []
    for n, (pg, ph) in enumerate(peers):
        copy = pltpu.make_async_remote_copy(
            lbuf.at[0], lbuf.at[n + 1], lsend.at[n], lrecv.at[n],
            device_id={"grp": pg, "head": ph}, device_id_type=MESH,
        )
        copy.start()
        loss_copies.append(copy)

    def up(c, dev, slot):
        return pltpu.make_async_remote_copy(
            sbuf.at[c], rbuf.at[slot, c], rsend.at[c], rrecv.at[slot, c],
            device_id={"seq": dev}, device_id_type=MESH,
        )

    for c in order:
        tree = (c // 2) % 2
        for slot, dev, cond in kids[tree]:

            @pl.when(cond)
            def _():
                up(c, dev, slot).wait_recv()
                sink[c] += rbuf[slot, c].astype(F32)

        @pl.when(jnp.logical_not(is_root))
        def _():
            sbuf[c] = sink[c].astype(BF16)
            dev, slot = parents[tree]
            up(c, dev, slot).start()

        if c == order[0]:

            @pl.when(seq > 0)
            def _():
                back.start()

    @pl.when(seq < nseq - 1)
    def _():
        back.wait_recv()
        acc_k[pl.ds(NB, WIN - 1)] += hr[0].astype(F32)
        acc_v[pl.ds(NB, WIN - 1)] += hr[1].astype(F32)

    @pl.when(is_root)
    def _():
        acc_k[pl.ds(WIN - 1, NB)] += sink[pl.ds(0, NGLOB)]
        acc_v[pl.ds(WIN - 1, NB)] += sink[pl.ds(NGLOB, NGLOB)]

    for b in range(NB):
        kgrad[b] = acc_k[b + WIN - 1].T.astype(BF16)
        vgrad[b] = acc_v[b + WIN - 1].T.astype(BF16)

    total = lbuf[0]
    for n, copy in enumerate(loss_copies):
        copy.wait_recv()
        total = total + lbuf[n + 1]
    loss_out[...] = total

    for b in range(NB):
        pltpu.make_async_copy(qg_v.at[b], qg_h.at[b], osem.at[b]).wait()
    for copy in loss_copies:
        copy.wait_send()

    @pl.when(seq > 0)
    def _():
        back.wait_send()

    @pl.when(seq < nseq - 1)
    def _():
        for copy in halo:
            copy.wait_send()

    for c in order:
        tree = (c // 2) % 2
        for slot, dev, cond in kids[tree]:

            @pl.when(cond)
            def _():
                bcast(c, slot, dev).wait_send()

        @pl.when(jnp.logical_not(is_root))
        def _():
            dev, slot = parents[tree]
            up(c, dev, slot).wait_send()


def local(queries, key_rows, values, out_grad, teacher_window, teacher_global, global_picks, mix_weight):
    nseq, ngrp, nhead = (lax.axis_size(a) for a in ("seq", "grp", "head"))
    width = HEADS * E
    hbm = pl.BlockSpec(memory_space=pl.ANY)
    vmem = pl.BlockSpec(memory_space=pltpu.VMEM)
    smem = pl.BlockSpec(memory_space=pltpu.SMEM)
    dma = pltpu.SemaphoreType.DMA
    npeer = max(ngrp * nhead - 1, 1)
    tile = (BLK, E)
    scratch = [
        pltpu.VMEM((NB, BLK, width), BF16),
        pltpu.VMEM((NB, BLK, width), BF16),
        pltpu.VMEM((NB, WIN, HEADS, BLK, BLK), BF16),
        pltpu.VMEM((NB, SLOTS - WIN, HEADS, BLK, BLK), BF16),
        pltpu.VMEM((len(CROSS), HEADS, BLK, BLK), BF16),
        pltpu.VMEM((NB + WIN - 1,) + tile, BF16),
        pltpu.VMEM((NB + WIN - 1,) + tile, BF16),
        pltpu.VMEM((CHUNKS,) + tile, BF16),
        pltpu.VMEM((SLOTS * BLK, E), BF16),
        pltpu.VMEM((SLOTS * BLK, E), BF16),
        pltpu.VMEM((2 * BLK, SLOTS * BLK), F32),
        pltpu.VMEM((2 * BLK, SLOTS * BLK), F32),
        pltpu.VMEM((2 * BLK, SLOTS * BLK), BF16),
        pltpu.VMEM((2 * BLK, SLOTS * BLK), BF16),
        pltpu.VMEM((E, SLOTS * BLK), F32),
        pltpu.VMEM((E, SLOTS * BLK), F32),
        pltpu.VMEM((NB, BLK, BLK), F32),
        pltpu.VMEM((BLK, BLK), F32),
        pltpu.VMEM((npeer + 1, NB, BLK), F32),
        pltpu.VMEM((NB + WIN - 1,) + tile, F32),
        pltpu.VMEM((NB + WIN - 1,) + tile, F32),
        pltpu.VMEM((CHUNKS,) + tile, F32),
        pltpu.VMEM((NB, BLK, width), BF16),
        pltpu.VMEM((CHUNKS,) + tile, BF16),
        pltpu.VMEM((4, CHUNKS) + tile, BF16),
        pltpu.VMEM((2, WIN - 1) + tile, BF16),
        pltpu.VMEM((2, WIN - 1) + tile, BF16),
        dma((32,)),
        dma((5,)),
        dma((5,)),
        dma((4, CHUNKS)),
        dma((CHUNKS,)),
        dma((CHUNKS,)),
        dma((4, CHUNKS)),
        dma((1,)),
        dma((1,)),
        dma((npeer,)),
        dma((npeer,)),
        dma((NB,)),
    ]
    out = pl.pallas_call(
        functools.partial(kernel, nseq, ngrp, nhead),
        out_shape=(
            jax.ShapeDtypeStruct((NB, BLK, width), BF16),
            jax.ShapeDtypeStruct((NB, BLK, E), BF16),
            jax.ShapeDtypeStruct((NB, BLK, E), BF16),
            jax.ShapeDtypeStruct((NB, BLK), F32),
        ),
        in_specs=[hbm] * 6 + [smem, vmem],
        out_specs=(hbm, vmem, vmem, vmem),
        scratch_shapes=scratch,
        compiler_params=pltpu.CompilerParams(
            collective_id=0, has_side_effects=True, vmem_limit_bytes=48 * 1024 * 1024
        ),
        name="distill_backward",
    )(
        queries.reshape(NB, BLK, width),
        key_rows.reshape(NB, BLK, E),
        values.reshape(NB, BLK, E),
        out_grad.reshape(NB, BLK, width),
        teacher_window,
        teacher_global,
        global_picks,
        mix_weight.reshape(NB, BLK),
    )
    query_grad, key_grad, value_grad, row_loss = out
    return (
        query_grad.reshape(NB * BLK, width),
        key_grad.reshape(NB * BLK, E),
        value_grad.reshape(NB * BLK, E),
        row_loss.reshape(NB * BLK),
    )


def solution(mesh):
    placed = (
        P("seq", ("grp", "head")),
        P("seq", ("grp", "head")),
        P("seq", ("grp", "head")),
        P("seq", ("grp", "head")),
        P("seq", None, ("grp", "head"), None, None),
        P("seq", None, ("grp", "head"), None, None),
        P("seq", None),
        P("seq"),
    )
    return jax.shard_map(
        local,
        mesh=mesh,
        in_specs=placed,
        out_specs=(
            P("seq", ("grp", "head")),
            P("seq", ("grp", "head")),
            P("seq", ("grp", "head")),
            P("seq"),
        ),
        check_vma=False,
    )
```

time: 188 us -> 105 us (0.56); the launches traced: 186 us -> 105 us
  Pallas kernels: 0 us -> 94.1 us
  starting transfers between devices: 51 us -> 0 us
  local copies, waits for them, and re-layouts: 51 us -> 10.2 us
  other arithmetic: 32.3 us -> 0 us
  matrix products: 25.5 us -> 0 us
  waiting for transfers between devices: 24.5 us -> 0 us
    pallas_call x0 -> x1, Pallas kernels: none -> 94.1 us  [local(): pl.pallas_call(functools.partial(kernel, nseq, ngrp, nhead), out_shape=(j...]
    all_to_all x5 -> x0, starting transfers between devices: 40.6 us -> none  [the longest x3 21.2 us: sent_to_all(): return lax.all_to_all(copies, axis, split_axis=0, concat_axis=0, tiled=True)]
    dot_general x5 -> x0, matrix products: 25.5 us -> none  [the longest x1 12 us: block_terms(): jnp.einsum('bqnge,bsjne->bsngqj', grad_tiles, value_cat, preferred_elemen...]
    all_to_all x5 -> x0, waiting for transfers between devices: 24.5 us -> none  [the longest x1 14 us: sum_at_owner_2(): lax.all_to_all(blocks, axis, split_axis=0, concat_axis=0, tiled=True)]
    convert_element_type x5 -> x0, other arithmetic: 15.2 us -> none  [the longest x1 12.1 us: block_terms(): score_low = score_grad.astype(jnp.bfloat16)]
    unnamed x62 -> x17, local copies, waits for them, and re-layouts: 22 us -> 10.2 us
    ppermute x3 -> x0, starting transfers between devices: 10.4 us -> none  [passed_along(): return lax.ppermute(block, axis, route)]
    another operation x8 -> x0, local copies, waits for them, and re-layouts: 8.96 us -> none  [the longest x2 4.21 us: local(): jnp.stack(window_tiles).reshape(blocks_here, WIN, heads_here, BLK, BLK)]
  transfers between devices with their start and end apart: 8 -> 0, of which waited for: 3 -> 0; matrix products, arithmetic and copies ran while one was open for 28% -> 0% of each run, Pallas kernels for 0% -> 0%
where the time goes in v1:
time: 105 us
  Pallas kernels  94.1 us (90%)
  local copies, waits for them, and re-layouts  10.2 us (10%)
    pallas_call x1, Pallas kernels, local(): pl.pallas_call(functools.partial(kernel, nseq, ngrp, nhead), out_shape=(j...  94.1 us
    unnamed x17, local copies, waits for them, and re-layouts  10.2 us

profile of v1, /device:TPU:4, one launch (start us, length us, event | category | flops | bytes accessed | tf_op | source)
XLA Modules:
  0.0 104.9 jit_solution(4292434815991443681)
XLA Ops:
  0.6 0.8 copy.12.picks
  1.4 0.0 copy-start
  1.4 1.6 %copy-done = bf16[4,2,8,128,128]{4,3,2,1,0:T(8,128)(2,1)S(1)} copy-done((bf16[4,2,8,128,128]{4,3,2,1,0:T(8,128)(2,1)S(1)}, bf16[4,2,8,128,128]{4,3,2,1,0:T(8,128)(2,1)}, u32[]{:S(2)}) %copy-start) | copy-done | bytes 2097176
  3.0 0.0 copy-start.1
  3.0 1.2 %copy-done.1 = bf16[512,1024]{1,0:T(8,128)(2,1)S(1)} copy-done((bf16[512,1024]{1,0:T(8,128)(2,1)S(1)}, bf16[512,1024]{1,0:T(8,128)(2,1)}, u32[]{:S(2)}) %copy-start.1) | copy-done | bytes 1048600
  4.2 0.0 copy-start.2
  4.2 1.2 %copy-done.2 = bf16[512,1024]{1,0:T(8,128)(2,1)S(1)} copy-done((bf16[512,1024]{1,0:T(8,128)(2,1)S(1)}, bf16[512,1024]{1,0:T(8,128)(2,1)}, u32[]{:S(2)}) %copy-start.2) | copy-done | bytes 1048600
  5.4 0.0 copy-start.3
  5.4 0.9 copy-done.3
  6.3 0.0 copy-start.4
  6.3 0.9 copy-done.4
  7.2 0.0 copy-start.5
  7.2 0.7 copy-done.5
  7.9 94.1 %distill_backward.1 = (bf16[4,128,1024]{2,1,0:T(8,128)(2,1)S(1)}, bf16[4,128,128]{2,1,0:T(8,128)(2,1)S(1)}, bf16[4,128,128]{2,1,0:T(8,128)(2,1)S(1)}, f32[4,128]{1,0:T(4,128)S(1)}) custom-call(bf16[4,128,1024]{2,1,0:T(8,128)(2,1)S(1)} %bitcast.9, bf16[4,128,128]{2,1,0:T(8,128)(2,1)S(1)} %bitcast.12, bf16[4,128,128]{2,1,0:T(8,128)(2,1)S(1)} %bitcast.13, ...), custom_call_target="tpu_custom_call" | custom-call | tf_op jit(solution)/shard_map/distill_backward/pallas_call | solution.py:444
  102.0 1.0 copy.17
  103.0 0.7 copy.18
  103.7 0.7 copy.19
  104.3 0.6 copy.20
Async XLA Ops:
  1.4 1.6 %copy-start = (bf16[4,2,8,128,128]{4,3,2,1,0:T(8,128)(2,1)S(1)}, bf16[4,2,8,128,128]{4,3,2,1,0:T(8,128)(2,1)}, u32[]{:S(2)}) copy-start(bf16[4,2,8,128,128]{4,3,2,1,0:T(8,128)(2,1)} %tg_h.1) | copy-start | bytes 6291460
  3.0 1.2 %copy-start.1 = (bf16[512,1024]{1,0:T(8,128)(2,1)S(1)}, bf16[512,1024]{1,0:T(8,128)(2,1)}, u32[]{:S(2)}) copy-start(bf16[512,1024]{1,0:T(8,128)(2,1)} %param.8) | copy-start | bytes 3145732
  4.2 1.2 %copy-start.2 = (bf16[512,1024]{1,0:T(8,128)(2,1)S(1)}, bf16[512,1024]{1,0:T(8,128)(2,1)}, u32[]{:S(2)}) copy-start(bf16[512,1024]{1,0:T(8,128)(2,1)} %param.11) | copy-start | bytes 3145732
  5.4 0.9 copy-start.3
  6.3 0.9 copy-start.4
  7.2 0.7 copy-start.5

commit v2 on v1

--- a/solution.py
+++ b/solution.py
@@ -25,55 +25,34 @@
 BF16 = jnp.bfloat16
 CHUNKS = 2 * NGLOB
 LOCAL_TILES = [(c, d) for c in range(NB) for d in range(WIN) if c + d < NB]
+HALO_A = [0, 1, 2]
+HALO_B = [3, 4]
 CROSS = [(3, 2), (3, 1), (2, 2)]
-
-
-def split_of(size):
-    z = 1
-    while size % z or size // z > z:
-        z += 1
-    return size // z, z
 
 
 def kernel(
     nseq, ngrp, nhead,
-    q_h, k_h, v_h, do_h, tw_h, tg_h, picks, mix_ref,
+    q_h, k_h, v_h, do_h, tw_h, tg_h, picks, mix_h,
     qg_h, kgrad, vgrad, loss_out,
-    q_v, do_v, tw_v, tg_v, th_v, k_v, v_v, glob, kc, vc,
-    s_scr, dp_scr, sg_scr, p_scr, dkt, dvt, mixc, loss_scr, lbuf,
-    acc_k, acc_v, sink, qg_v, sbuf, rbuf, hs, hr,
+    q_v, do_v, tw_v, tg_v, th_v, k_v, v_v, glob, glob_kv, kc, vc,
+    s_scr, dp_scr, sg_scr, p_scr, dkt, dvt, mix_ref, mixc, loss_scr, lbuf,
+    acc_k, acc_v, sink, qg_v, sbuf, rbuf, tsum, hs, hr,
     lsem, hsend, hrecv, bsend, brecv, rsend, rrecv, gsend, grecv, lsend, lrecv, osem,
 ):
-    ny, nz = split_of(nseq)
     seq = lax.axis_index("seq")
     grp = lax.axis_index("grp")
     head = lax.axis_index("head")
-    y = seq // nz
-    z = seq % nz
-    zhalf, yhalf = nz // 2, ny // 2
-    z_up, z_dn = lax.rem(z + 1, nz), lax.rem(z + nz - 1, nz)
-    y_up, y_dn = lax.rem(y + 1, ny), lax.rem(y + ny - 1, ny)
-    dev_zu, dev_zd = y * nz + z_up, y * nz + z_dn
-    dev_yu, dev_yd = y_up * nz + z, y_dn * nz + z
-    nxt, prv = lax.rem(seq + 1, nseq), lax.rem(seq + nseq - 1, nseq)
-    kid_zu = (z < zhalf) if nz > 1 else (z < 0)
-    kid_zd = ((z == 0) | (z > zhalf + 1)) if nz > 2 else (z < 0)
-    kid_yu = (y < yhalf) if ny > 1 else (y < 0)
-    kid_yd = ((y == 0) | (y > yhalf + 1)) if ny > 2 else (y < 0)
-    kids = [
-        [(0, dev_zu, kid_zu), (1, dev_zd, kid_zd), (2, dev_yu, kid_yu & (z == 0)), (3, dev_yd, kid_yd & (z == 0))],
-        [(0, dev_zu, kid_zu & (y == 0)), (1, dev_zd, kid_zd & (y == 0)), (2, dev_yu, kid_yu), (3, dev_yd, kid_yd)],
-    ]
-    z_low = z <= zhalf
-    y_low = y <= yhalf
-    z_par = jnp.where(z_low, dev_zd, dev_zu)
-    z_slot = jnp.where(z_low, 0, 1)
-    y_par = jnp.where(y_low, dev_yd, dev_yu)
-    y_slot = jnp.where(y_low, 2, 3)
-    parents = [
-        (jnp.where(z > 0, z_par, y_par), jnp.where(z > 0, z_slot, y_slot)),
-        (jnp.where(y > 0, y_par, z_par), jnp.where(y > 0, y_slot, z_slot)),
-    ]
+    piece = CHUNKS * BLK // nseq
+    others = [lax.rem(seq + off, nseq) for off in range(1, nseq)]
+    nxt, prv = others[0], others[-1]
+
+    def rows_of(dev):
+        return pl.ds(pl.multiple_of(dev * piece, piece), piece)
+
+    def total_wait(ref, sem):
+        part = ref.at[pl.ds(0, (nseq - 1) * piece)]
+        pltpu.make_async_copy(part, part, sem).wait()
+
     is_root = seq == 0
 
     loads = {}
@@ -85,8 +64,9 @@
         copy.start()
         loads.setdefault(key, []).append(copy)
 
-    load("kv", k_h, k_v.at[pl.ds(WIN - 1, NB)])
-    load("kv", v_h, v_v.at[pl.ds(WIN - 1, NB)])
+    load("mix", mix_h, mix_ref)
+    load("kv", k_h, k_v.at[pl.ds((WIN - 1) * BLK, NB * BLK)])
+    load("kv", v_h, v_v.at[pl.ds((WIN - 1) * BLK, NB * BLK)])
     for b in reversed(range(NB)):
         load(b, q_h.at[b], q_v.at[b])
         load(b, do_h.at[b], do_v.at[b])
@@ -96,10 +76,14 @@
         load(b, tg_h.at[b], tg_v.at[b])
 
     barrier = pltpu.get_barrier_semaphore()
-    waits = 0
-    for dev in (dev_zu, dev_zd, dev_yu, dev_yd, nxt, prv):
+    waits = 2
+    for dev in (nxt, prv):
         pl.semaphore_signal(barrier, inc=1, device_id={"seq": dev}, device_id_type=MESH)
-        waits += 1
+
+    @pl.when(jnp.logical_not(is_root))
+    def _():
+        pl.semaphore_signal(barrier, inc=1, device_id={"seq": 0}, device_id_type=MESH)
+
     peers = []
     for off in range(1, ngrp * nhead):
         flat = lax.rem(grp * nhead + head + off, ngrp * nhead)
@@ -107,13 +91,20 @@
     for pg, ph in peers:
         pl.semaphore_signal(barrier, inc=1, device_id={"grp": pg, "head": ph}, device_id_type=MESH)
         waits += 1
-    pl.semaphore_wait(barrier, waits)
+
+    @pl.when(jnp.logical_not(is_root))
+    def _():
+        pl.semaphore_wait(barrier, waits)
+
+    @pl.when(is_root)
+    def _():
+        pl.semaphore_wait(barrier, waits + nseq - 1)
 
     def halo_copies():
         out = []
         ends = [
-            (k_h.at[pl.ds(NB - WIN + 1, WIN - 1)], k_v.at[pl.ds(0, WIN - 1)]),
-            (v_h.at[pl.ds(NB - WIN + 1, WIN - 1)], v_v.at[pl.ds(0, WIN - 1)]),
+            (k_h.at[pl.ds((NB - WIN + 1) * BLK, (WIN - 1) * BLK)], k_v.at[pl.ds(0, (WIN - 1) * BLK)]),
+            (v_h.at[pl.ds((NB - WIN + 1) * BLK, (WIN - 1) * BLK)], v_v.at[pl.ds(0, (WIN - 1) * BLK)]),
         ] + [(tw_h.at[c, d], th_v.at[i]) for i, (c, d) in enumerate(CROSS)]
         for i, (src, dst) in enumerate(ends):
             out.append(
@@ -125,45 +116,44 @@
 
     halo = halo_copies()
 
-    @pl.when(seq < nseq - 1)
-    def _():
-        for copy in halo:
-            copy.start()
-
-    def bcast(c, slot, dev):
-        return pltpu.make_async_remote_copy(
-            glob.at[c], glob.at[c], bsend.at[slot, c], brecv.at[c],
-            device_id={"seq": dev}, device_id_type=MESH,
-        )
+    def halo_start(indices):
+        @pl.when(seq < nseq - 1)
+        def _():
+            for i in indices:
+                halo[i].start()
 
     @pl.when(is_root)
     def _():
-        a = pltpu.make_async_copy(k_h, glob.at[pl.ds(0, NGLOB)], lsem.at[count[0]])
-        b = pltpu.make_async_copy(v_h, glob.at[pl.ds(NGLOB, NGLOB)], lsem.at[count[0] + 1])
-        a.start()
-        b.start()
-        k_v[pl.ds(0, WIN - 1)] = jnp.zeros((WIN - 1, BLK, E), BF16)
-        v_v[pl.ds(0, WIN - 1)] = jnp.zeros((WIN - 1, BLK, E), BF16)
+        half = nseq // 2
+        for dev in range(nseq):
+            src = (k_h if dev < half else v_h).at[pl.ds((dev % half) * piece, piece)]
+            dst = glob.at[pl.ds(dev * piece, piece)]
+            if dev:
+                pltpu.make_async_remote_copy(
+                    src, dst, bsend.at[0], brecv.at[0], device_id={"seq": dev}, device_id_type=MESH
+                ).start()
+            else:
+                pltpu.make_async_copy(src, dst, brecv.at[0]).start()
+        k_v[pl.ds(0, (WIN - 1) * BLK)] = jnp.zeros(((WIN - 1) * BLK, E), BF16)
+        v_v[pl.ds(0, (WIN - 1) * BLK)] = jnp.zeros(((WIN - 1) * BLK, E), BF16)
         th_v[...] = jnp.zeros_like(th_v)
-        a.wait()
-        b.wait()
-
-    order = [0, 2, 1, 3, 4, 6, 5, 7]
-    for c in order:
-        tree = (c // 2) % 2
-
-        @pl.when(jnp.logical_not(is_root))
-        def _():
-            bcast(c, 0, parents[tree][0]).wait_recv()
-
-        for slot, dev, cond in kids[tree]:
-
-            @pl.when(cond)
-            def _():
-                bcast(c, slot, dev).start()
-
+
+    halo_start(HALO_A)
+    mine = glob.at[rows_of(seq)]
+    pltpu.make_async_copy(mine, mine, brecv.at[0]).wait()
+    for dev in others:
+        pltpu.make_async_remote_copy(
+            mine, mine, bsend.at[1], brecv.at[1], device_id={"seq": dev}, device_id_type=MESH
+        ).start()
+    halo_start(HALO_B)
+
+    for copy in loads["mix"]:
+        copy.wait()
     for b in range(NB):
         mixc[b] = jnp.broadcast_to(mix_ref[pl.ds(b, 1), :], (BLK, BLK)).T
+    total_wait(glob, brecv.at[1])
+    for n in range(CHUNKS):
+        glob_kv[n] = glob[pl.ds(n * BLK, BLK), :]
     acc_k[...] = jnp.zeros_like(acc_k)
     acc_v[...] = jnp.zeros_like(acc_v)
     sink[...] = jnp.zeros_like(sink)
@@ -190,17 +180,17 @@
         for copy in loads[b]:
             copy.wait()
         for d in range(WIN):
-            kc[pl.ds(d * BLK, BLK), :] = k_v[b + WIN - 1 - d]
-            vc[pl.ds(d * BLK, BLK), :] = v_v[b + WIN - 1 - d]
+            kc[pl.ds(d * BLK, BLK), :] = k_v[pl.ds((b + WIN - 1 - d) * BLK, BLK), :]
+            vc[pl.ds(d * BLK, BLK), :] = v_v[pl.ds((b + WIN - 1 - d) * BLK, BLK), :]
         biases = [None] * SLOTS
         for d in range(1, WIN):
             if b < d:
                 biases[d] = jnp.where(seq > 0, 0.0, NEG)
         for g in range(SLOTS - WIN):
-            pick = picks[b, g]
+            pick = picks[g, b]
             safe = jnp.maximum(pick, 0)
-            kc[pl.ds((WIN + g) * BLK, BLK), :] = glob[safe]
-            vc[pl.ds((WIN + g) * BLK, BLK), :] = glob[safe + NGLOB]
+            kc[pl.ds((WIN + g) * BLK, BLK), :] = glob_kv[safe]
+            vc[pl.ds((WIN + g) * BLK, BLK), :] = glob_kv[safe + NGLOB]
             biases[WIN + g] = jnp.where(pick >= 0, 0.0, NEG)
         tiles = []
         for d in range(WIN):
@@ -290,21 +280,32 @@
             acc_k[b + WIN - 1 - d] += dkt[:, pl.ds(d * BLK, BLK)] * SCALE
             acc_v[b + WIN - 1 - d] += dvt[:, pl.ds(d * BLK, BLK)]
         for g in range(SLOTS - WIN):
-            pick = picks[b, g]
+            pick = picks[g, b]
             for n in range(NGLOB):
                 hit = jnp.where(pick == n, 1.0, 0.0)
-                sink[n] += dkt[:, pl.ds((WIN + g) * BLK, BLK)] * (hit * SCALE)
-                sink[NGLOB + n] += dvt[:, pl.ds((WIN + g) * BLK, BLK)] * hit
+                sink[pl.ds(n * BLK, BLK), :] += dkt[:, pl.ds((WIN + g) * BLK, BLK)] * (hit * SCALE)
+                sink[pl.ds((NGLOB + n) * BLK, BLK), :] += dvt[:, pl.ds((WIN + g) * BLK, BLK)] * hit
         lbuf[0, pl.ds(b, 1), :] = loss_scr[...].T[0:1, :]
 
     for b in reversed(range(NB)):
         block(b)
 
+    sbuf[...] = sink[...].astype(BF16)
     hs[0] = acc_k[pl.ds(0, WIN - 1)].astype(BF16)
     hs[1] = acc_v[pl.ds(0, WIN - 1)].astype(BF16)
+    for n, dev in enumerate(others):
+        pltpu.make_async_remote_copy(
+            sbuf.at[rows_of(dev)], rbuf.at[pl.ds(n * piece, piece)], rsend.at[0], rrecv.at[0],
+            device_id={"seq": dev}, device_id_type=MESH,
+        ).start()
+
     back = pltpu.make_async_remote_copy(
         hs, hr, gsend.at[0], grecv.at[0], device_id={"seq": prv}, device_id_type=MESH
     )
+
+    @pl.when(seq > 0)
+    def _():
+        back.start()
 
     loss_copies = []
     for n, (pg, ph) in enumerate(peers):
@@ -315,32 +316,19 @@
         copy.start()
         loss_copies.append(copy)
 
-    def up(c, dev, slot):
-        return pltpu.make_async_remote_copy(
-            sbuf.at[c], rbuf.at[slot, c], rsend.at[c], rrecv.at[slot, c],
-            device_id={"seq": dev}, device_id_type=MESH,
-        )
-
-    for c in order:
-        tree = (c // 2) % 2
-        for slot, dev, cond in kids[tree]:
-
-            @pl.when(cond)
-            def _():
-                up(c, dev, slot).wait_recv()
-                sink[c] += rbuf[slot, c].astype(F32)
-
-        @pl.when(jnp.logical_not(is_root))
-        def _():
-            sbuf[c] = sink[c].astype(BF16)
-            dev, slot = parents[tree]
-            up(c, dev, slot).start()
-
-        if c == order[0]:
-
-            @pl.when(seq > 0)
-            def _():
-                back.start()
+    total_wait(rbuf, rrecv.at[0])
+    summed = sink[rows_of(seq), :]
+    for n in range(nseq - 1):
+        summed = summed + rbuf[pl.ds(n * piece, piece), :].astype(F32)
+    tsum[rows_of(seq), :] = summed.astype(BF16)
+    give = pltpu.make_async_remote_copy(
+        tsum.at[rows_of(seq)], tsum.at[rows_of(seq)], rsend.at[1], rrecv.at[1],
+        device_id={"seq": 0}, device_id_type=MESH,
+    )
+
+    @pl.when(jnp.logical_not(is_root))
+    def _():
+        give.start()
 
     @pl.when(seq < nseq - 1)
     def _():
@@ -350,8 +338,10 @@
 
     @pl.when(is_root)
     def _():
-        acc_k[pl.ds(WIN - 1, NB)] += sink[pl.ds(0, NGLOB)]
-        acc_v[pl.ds(WIN - 1, NB)] += sink[pl.ds(NGLOB, NGLOB)]
+        total_wait(tsum, rrecv.at[1])
+        for n in range(NGLOB):
+            acc_k[WIN - 1 + n] += tsum[pl.ds(n * BLK, BLK), :].astype(F32)
+            acc_v[WIN - 1 + n] += tsum[pl.ds((NGLOB + n) * BLK, BLK), :].astype(F32)
 
     for b in range(NB):
         kgrad[b] = acc_k[b + WIN - 1].T.astype(BF16)
@@ -377,26 +367,23 @@
         for copy in halo:
             copy.wait_send()
 
-    for c in order:
-        tree = (c // 2) % 2
-        for slot, dev, cond in kids[tree]:
-
-            @pl.when(cond)
-            def _():
-                bcast(c, slot, dev).wait_send()
-
-        @pl.when(jnp.logical_not(is_root))
-        def _():
-            dev, slot = parents[tree]
-            up(c, dev, slot).wait_send()
+    total_wait(glob, bsend.at[1])
+    total_wait(sbuf, rsend.at[0])
+
+    @pl.when(is_root)
+    def _():
+        total_wait(glob, bsend.at[0])
+
+    @pl.when(jnp.logical_not(is_root))
+    def _():
+        give.wait_send()
 
 
 def local(queries, key_rows, values, out_grad, teacher_window, teacher_global, global_picks, mix_weight):
     nseq, ngrp, nhead = (lax.axis_size(a) for a in ("seq", "grp", "head"))
     width = HEADS * E
-    hbm = pl.BlockSpec(memory_space=pl.ANY)
+    hbm = pl.BlockSpec(memory_space=pltpu.HBM)
     vmem = pl.BlockSpec(memory_space=pltpu.VMEM)
-    smem = pl.BlockSpec(memory_space=pltpu.SMEM)
     dma = pltpu.SemaphoreType.DMA
     npeer = max(ngrp * nhead - 1, 1)
     tile = (BLK, E)
@@ -406,8 +393,9 @@
         pltpu.VMEM((NB, WIN, HEADS, BLK, BLK), BF16),
         pltpu.VMEM((NB, SLOTS - WIN, HEADS, BLK, BLK), BF16),
         pltpu.VMEM((len(CROSS), HEADS, BLK, BLK), BF16),
-        pltpu.VMEM((NB + WIN - 1,) + tile, BF16),
-        pltpu.VMEM((NB + WIN - 1,) + tile, BF16),
+        pltpu.VMEM(((NB + WIN - 1) * BLK, E), BF16),
+        pltpu.VMEM(((NB + WIN - 1) * BLK, E), BF16),
+        pltpu.VMEM((CHUNKS * BLK, E), BF16),
         pltpu.VMEM((CHUNKS,) + tile, BF16),
         pltpu.VMEM((SLOTS * BLK, E), BF16),
         pltpu.VMEM((SLOTS * BLK, E), BF16),
@@ -417,24 +405,26 @@
         pltpu.VMEM((2 * BLK, SLOTS * BLK), BF16),
         pltpu.VMEM((E, SLOTS * BLK), F32),
         pltpu.VMEM((E, SLOTS * BLK), F32),
+        pltpu.VMEM((NB, BLK), F32),
         pltpu.VMEM((NB, BLK, BLK), F32),
         pltpu.VMEM((BLK, BLK), F32),
         pltpu.VMEM((npeer + 1, NB, BLK), F32),
         pltpu.VMEM((NB + WIN - 1,) + tile, F32),
         pltpu.VMEM((NB + WIN - 1,) + tile, F32),
-        pltpu.VMEM((CHUNKS,) + tile, F32),
+        pltpu.VMEM((CHUNKS * BLK, E), F32),
         pltpu.VMEM((NB, BLK, width), BF16),
-        pltpu.VMEM((CHUNKS,) + tile, BF16),
-        pltpu.VMEM((4, CHUNKS) + tile, BF16),
+        pltpu.VMEM((CHUNKS * BLK, E), BF16),
+        pltpu.VMEM((CHUNKS * BLK, E), BF16),
+        pltpu.VMEM((CHUNKS * BLK, E), BF16),
         pltpu.VMEM((2, WIN - 1) + tile, BF16),
         pltpu.VMEM((2, WIN - 1) + tile, BF16),
         dma((32,)),
         dma((5,)),
         dma((5,)),
-        dma((4, CHUNKS)),
-        dma((CHUNKS,)),
-        dma((CHUNKS,)),
-        dma((4, CHUNKS)),
+        dma((2,)),
+        dma((2,)),
+        dma((2,)),
+        dma((2,)),
         dma((1,)),
         dma((1,)),
         dma((npeer,)),
@@ -449,7 +439,7 @@
             jax.ShapeDtypeStruct((NB, BLK, E), BF16),
             jax.ShapeDtypeStruct((NB, BLK), F32),
         ),
-        in_specs=[hbm] * 6 + [smem, vmem],
+        in_specs=[hbm] * 6 + [pl.BlockSpec(memory_space=pltpu.SMEM), hbm],
         out_specs=(hbm, vmem, vmem, vmem),
         scratch_shapes=scratch,
         compiler_params=pltpu.CompilerParams(
@@ -457,14 +447,19 @@
         ),
         name="distill_backward",
     )(
-        queries.reshape(NB, BLK, width),
-        key_rows.reshape(NB, BLK, E),
-        values.reshape(NB, BLK, E),
-        out_grad.reshape(NB, BLK, width),
-        teacher_window,
-        teacher_global,
-        global_picks,
-        mix_weight.reshape(NB, BLK),
+        *(
+            pltpu.with_memory_space_constraint(x, pltpu.HBM)
+            for x in (
+                queries.reshape(NB, BLK, width),
+                key_rows,
+                values,
+                out_grad.reshape(NB, BLK, width),
+                teacher_window,
+                teacher_global,
+            )
+        ),
+        global_picks.T,
+        pltpu.with_memory_space_constraint(mix_weight.reshape(NB, BLK), pltpu.HBM),
     )
     query_grad, key_grad, value_grad, row_loss = out
     return (

time: 105 us -> 69.2 us (0.66)
  Pallas kernels: 94.1 us -> 64.8 us
  local copies, waits for them, and re-layouts: 10.2 us -> 3.53 us
    pallas_call x1, Pallas kernels: 94.1 us -> 64.8 us  [local(): pl.pallas_call(functools.partial(kernel, nseq, ngrp, nhead), out_shape=(j...]
    unnamed x17 -> x6, local copies, waits for them, and re-layouts: 10.2 us -> 3.53 us
where the time goes in v2:
time: 69.2 us; the launch traced here: 69 us
  Pallas kernels  64.8 us (94%)
  local copies, waits for them, and re-layouts  3.53 us (5%)
    pallas_call x1, Pallas kernels, local(): pl.pallas_call(functools.partial(kernel, nseq, ngrp, nhead), out_shape=(j...  64.8 us
    unnamed x6, local copies, waits for them, and re-layouts  3.53 us

profile of v2, /device:TPU:4, one launch (start us, length us, event | category | flops | bytes accessed | tf_op | source)
XLA Modules:
  0.0 69.0 jit_solution(9108328956336446144)
XLA Ops:
  0.6 0.0 copy-start
  0.6 0.7 copy-done
  1.3 64.8 %distill_backward.1 = (bf16[4,128,1024]{2,1,0:T(8,128)(2,1)S(1)}, bf16[4,128,128]{2,1,0:T(8,128)(2,1)S(1)}, bf16[4,128,128]{2,1,0:T(8,128)(2,1)S(1)}, f32[4,128]{1,0:T(4,128)S(1)}) custom-call(bf16[4,128,1024]{2,1,0:T(8,128)(2,1)} %bitcast.13, bf16[512,128]{1,0:T(8,128)(2,1)} %k_h.1, bf16[512,128]{1,0:T(8,128)(2,1)} %v_h.1, bf16[4,128,1024]{2,1,0:T(8,128)(2,1)} %bitcast.14, ...), custom_call_target="tpu_custom_call" | custom-call | tf_op jit(solution)/shard_map/distill_backward/pallas_call | solution.py:434
  66.1 1.0 %copy.16 = bf16[512,1024]{1,0:T(8,128)(2,1)} copy(bf16[512,1024]{1,0:T(8,128)(2,1)S(1)} %bitcast.8) | data formatting | bytes 2097152
  67.1 0.7 copy.17
  67.7 0.7 copy.18
  68.4 0.6 copy.19
Async XLA Ops:
  0.6 0.7 copy-start

commit v3 on v2

--- a/solution.py
+++ b/solution.py
@@ -25,8 +25,9 @@
 BF16 = jnp.bfloat16
 CHUNKS = 2 * NGLOB
 LOCAL_TILES = [(c, d) for c in range(NB) for d in range(WIN) if c + d < NB]
-HALO_A = [0, 1, 2]
-HALO_B = [3, 4]
+HALO_A = [0, 1]
+HALO_B = [2, 3, 4]
+UNROLL = 4
 CROSS = [(3, 2), (3, 1), (2, 2)]
 
 
@@ -204,20 +205,26 @@
         dvt[...] = jnp.zeros_like(dvt)
         loss_scr[...] = jnp.zeros_like(loss_scr)
 
-        def pair(i, carry):
+        def operands(i):
             h0 = 2 * i
             lanes = [pl.ds(pl.multiple_of((h0 + e) * E, E), E) for e in range(2)]
             q2 = jnp.concatenate([q_v[b, :, lanes[0]], q_v[b, :, lanes[1]]], axis=0)
             do2 = jnp.concatenate([do_v[b, :, lanes[0]], do_v[b, :, lanes[1]]], axis=0)
-            keys = kc[...]
-            s_scr[...] = lax.dot_general(q2, keys, dims_t, preferred_element_type=F32)
-            dp_scr[...] = lax.dot_general(do2, vc[...], dims_t, preferred_element_type=F32)
+            return lanes, q2, do2
+
+        def forward(i, k):
+            lanes, q2, do2 = operands(i)
+            s_scr[k] = lax.dot_general(q2, kc[...], dims_t, preferred_element_type=F32)
+            dp_scr[k] = lax.dot_general(do2, vc[...], dims_t, preferred_element_type=F32)
+
+        def middle(i, k):
+            h0 = 2 * i
             for n in range(2 * BLK // ROWS):
                 e, r0 = n // (BLK // ROWS), (n % (BLK // ROWS)) * ROWS
                 at = pl.ds(n * ROWS, ROWS)
                 ss, ts = [], []
                 for j in range(SLOTS):
-                    s = s_scr[at, pl.ds(j * BLK, BLK)] * (SCALE * LOG2E)
+                    s = s_scr[k, at, pl.ds(j * BLK, BLK)] * (SCALE * LOG2E)
                     t = tiles[j][h0 + e, pl.ds(r0, ROWS), :].astype(F32) * LOG2E
                     if j == 0:
                         live = col <= row + r0
@@ -240,7 +247,7 @@
                     e_s = jnp.exp2(sp)
                     e_t = jnp.exp2(tp)
                     u = sp - tp
-                    x = other * u + dp_scr[at, pl.ds(j * BLK, BLK)]
+                    x = other * u + dp_scr[k, at, pl.ds(j * BLK, BLK)]
                     terms = (e_s, e_t, e_t * u, e_s * u, e_s * x)
                     if j == 0:
                         z_s, z_t, f_u, r_u, x_u = terms
@@ -264,17 +271,34 @@
                 t_fac = mix * i_t
                 for j in range(SLOTS):
                     p = es[j] * i_s
-                    p_scr[at, pl.ds(j * BLK, BLK)] = p.astype(BF16)
-                    sg_scr[at, pl.ds(j * BLK, BLK)] = (p * (xs[j] + shift) - t_fac * et[j]).astype(BF16)
-            sg = sg_scr[...]
-            qg = (jnp.dot(sg, keys, preferred_element_type=F32) * SCALE).astype(BF16)
+                    p_scr[k, at, pl.ds(j * BLK, BLK)] = p.astype(BF16)
+                    sg_scr[k, at, pl.ds(j * BLK, BLK)] = (p * (xs[j] + shift) - t_fac * et[j]).astype(BF16)
+
+        def backward(i, k):
+            lanes, q2, do2 = operands(i)
+            sg = sg_scr[k]
+            qg = (jnp.dot(sg, kc[...], preferred_element_type=F32) * SCALE).astype(BF16)
             qg_v[b, :, lanes[0]] = qg[:BLK]
             qg_v[b, :, lanes[1]] = qg[BLK:]
             dkt[...] += lax.dot_general(q2, sg, dims_c, preferred_element_type=F32)
-            dvt[...] += lax.dot_general(do2, p_scr[...], dims_c, preferred_element_type=F32)
+            dvt[...] += lax.dot_general(do2, p_scr[k], dims_c, preferred_element_type=F32)
+
+        def pairs(step, carry):
+            base = step * UNROLL
+            forward(base, 0)
+            for k in range(UNROLL):
+                if k + 1 < UNROLL:
+                    forward(base + k + 1, k + 1)
+                middle(base + k, k)
+                if k:
+                    backward(base + k - 1, k - 1)
+            backward(base + UNROLL - 1, UNROLL - 1)
             return carry
 
-        lax.fori_loop(0, HEADS // 2, pair, 0)
+        if UNROLL == HEADS // 2:
+            pairs(0, 0)
+        else:
+            lax.fori_loop(0, HEADS // 2 // UNROLL, pairs, 0)
         pltpu.make_async_copy(qg_v.at[b], qg_h.at[b], osem.at[b]).start()
         for d in range(WIN):
             acc_k[b + WIN - 1 - d] += dkt[:, pl.ds(d * BLK, BLK)] * SCALE
@@ -399,10 +423,10 @@
         pltpu.VMEM((CHUNKS,) + tile, BF16),
         pltpu.VMEM((SLOTS * BLK, E), BF16),
         pltpu.VMEM((SLOTS * BLK, E), BF16),
-        pltpu.VMEM((2 * BLK, SLOTS * BLK), F32),
-        pltpu.VMEM((2 * BLK, SLOTS * BLK), F32),
-        pltpu.VMEM((2 * BLK, SLOTS * BLK), BF16),
-        pltpu.VMEM((2 * BLK, SLOTS * BLK), BF16),
+        pltpu.VMEM((UNROLL, 2 * BLK, SLOTS * BLK), F32),
+        pltpu.VMEM((UNROLL, 2 * BLK, SLOTS * BLK), F32),
+        pltpu.VMEM((UNROLL, 2 * BLK, SLOTS * BLK), BF16),
+        pltpu.VMEM((UNROLL, 2 * BLK, SLOTS * BLK), BF16),
         pltpu.VMEM((E, SLOTS * BLK), F32),
         pltpu.VMEM((E, SLOTS * BLK), F32),
         pltpu.VMEM((NB, BLK), F32),

time: 69.2 us -> 63.8 us (0.922)
  Pallas kernels: 64.8 us -> 59.5 us
    pallas_call x1, Pallas kernels: 64.8 us -> 59.5 us  [local(): pl.pallas_call(functools.partial(kernel, nseq, ngrp, nhead), out_shape=(j...]
where the time goes in v3:
time: 63.8 us; the launch traced here: 63.7 us
  Pallas kernels  59.5 us (93%)
  local copies, waits for them, and re-layouts  3.53 us (6%)
  between operations  0.65 us (1%)
    pallas_call x1, Pallas kernels, local(): pl.pallas_call(functools.partial(kernel, nseq, ngrp, nhead), out_shape=(j...  59.5 us
    unnamed x6, local copies, waits for them, and re-layouts  3.53 us

profile of v3, /device:TPU:4, one launch (start us, length us, event | category | flops | bytes accessed | tf_op | source)
XLA Modules:
  0.0 63.7 jit_solution(10353070958354131377)
XLA Ops:
  0.6 0.0 copy-start
  0.6 0.7 %copy-done = s32[4,2]{0,1:T(2,128)S(1)} copy-done((s32[4,2]{0,1:T(2,128)S(1)}, s32[4,2]{0,1:T(2,128)}, u32[]{:S(2)}) %copy-start) | copy-done | bytes 56
  1.3 59.5 %distill_backward.1 = (bf16[4,128,1024]{2,1,0:T(8,128)(2,1)S(1)}, bf16[4,128,128]{2,1,0:T(8,128)(2,1)S(1)}, bf16[4,128,128]{2,1,0:T(8,128)(2,1)S(1)}, f32[4,128]{1,0:T(4,128)S(1)}) custom-call(bf16[4,128,1024]{2,1,0:T(8,128)(2,1)} %bitcast.13, bf16[512,128]{1,0:T(8,128)(2,1)} %k_h.1, bf16[512,128]{1,0:T(8,128)(2,1)} %v_h.1, bf16[4,128,1024]{2,1,0:T(8,128)(2,1)} %bitcast.14, ...), custom_call_target="tpu_custom_call" | custom-call | tf_op jit(solution)/shard_map/distill_backward/pallas_call | solution.py:458
  60.8 1.0 %copy.16 = bf16[512,1024]{1,0:T(8,128)(2,1)} copy(bf16[512,1024]{1,0:T(8,128)(2,1)S(1)} %bitcast.8) | data formatting | bytes 2097152
  61.8 0.7 %copy.17 = bf16[512,128]{1,0:T(8,128)(2,1)} copy(bf16[512,128]{1,0:T(8,128)(2,1)S(1)} %bitcast.10) | data formatting | bytes 262144
  62.4 0.7 %copy.18 = bf16[512,128]{1,0:T(8,128)(2,1)} copy(bf16[512,128]{1,0:T(8,128)(2,1)S(1)} %bitcast.9) | data formatting | bytes 262144
  63.1 0.6 copy.19
Async XLA Ops:
  0.6 0.7 %copy-start = (s32[4,2]{0,1:T(2,128)S(1)}, s32[4,2]{0,1:T(2,128)}, u32[]{:S(2)}) copy-start(s32[4,2]{0,1:T(2,128)} %param.14) | copy-start | bytes 100

commit v4 on v3

--- a/solution.py
+++ b/solution.py
@@ -31,6 +31,13 @@
 CROSS = [(3, 2), (3, 1), (2, 2)]
 
 
+def ring_distance(off, nseq):
+    nz = min(nseq, 8)
+    ny = nseq // nz
+    y, z = off // nz, off % nz
+    return min(y, ny - y) + min(z, nz - z)
+
+
 def kernel(
     nseq, ngrp, nhead,
     q_h, k_h, v_h, do_h, tw_h, tg_h, picks, mix_h,
@@ -44,8 +51,9 @@
     grp = lax.axis_index("grp")
     head = lax.axis_index("head")
     piece = CHUNKS * BLK // nseq
-    others = [lax.rem(seq + off, nseq) for off in range(1, nseq)]
-    nxt, prv = others[0], others[-1]
+    by_distance = sorted(range(1, nseq), key=lambda off: -ring_distance(off, nseq))
+    others = [lax.rem(seq + off, nseq) for off in by_distance]
+    nxt, prv = lax.rem(seq + 1, nseq), lax.rem(seq + nseq - 1, nseq)
 
     def rows_of(dev):
         return pl.ds(pl.multiple_of(dev * piece, piece), piece)
@@ -126,7 +134,7 @@
     @pl.when(is_root)
     def _():
         half = nseq // 2
-        for dev in range(nseq):
+        for dev in by_distance + [0]:
             src = (k_h if dev < half else v_h).at[pl.ds((dev % half) * piece, piece)]
             dst = glob.at[pl.ds(dev * piece, piece)]
             if dev:
@@ -360,22 +368,22 @@
         acc_k[pl.ds(NB, WIN - 1)] += hr[0].astype(F32)
         acc_v[pl.ds(NB, WIN - 1)] += hr[1].astype(F32)
 
-    @pl.when(is_root)
-    def _():
-        total_wait(tsum, rrecv.at[1])
-        for n in range(NGLOB):
-            acc_k[WIN - 1 + n] += tsum[pl.ds(n * BLK, BLK), :].astype(F32)
-            acc_v[WIN - 1 + n] += tsum[pl.ds((NGLOB + n) * BLK, BLK), :].astype(F32)
-
-    for b in range(NB):
-        kgrad[b] = acc_k[b + WIN - 1].T.astype(BF16)
-        vgrad[b] = acc_v[b + WIN - 1].T.astype(BF16)
-
     total = lbuf[0]
     for n, copy in enumerate(loss_copies):
         copy.wait_recv()
         total = total + lbuf[n + 1]
     loss_out[...] = total
+
+    @pl.when(is_root)
+    def _():
+        total_wait(tsum, rrecv.at[1])
+        for n in range(NGLOB):
+            acc_k[WIN - 1 + n] += tsum[pl.ds(n * BLK, BLK), :].astype(F32)
+            acc_v[WIN - 1 + n] += tsum[pl.ds((NGLOB + n) * BLK, BLK), :].astype(F32)
+
+    for b in range(NB):
+        kgrad[b] = acc_k[b + WIN - 1].T.astype(BF16)
+        vgrad[b] = acc_v[b + WIN - 1].T.astype(BF16)
 
     for b in range(NB):
         pltpu.make_async_copy(qg_v.at[b], qg_h.at[b], osem.at[b]).wait()

time: 63.8 us -> 62.3 us (0.976)
  Pallas kernels: 59.5 us -> 57.7 us
    pallas_call x1, Pallas kernels: 59.5 us -> 57.7 us  [local(): pl.pallas_call(functools.partial(kernel, nseq, ngrp, nhead), out_shape=(j...]
where the time goes in v4:
time: 62.3 us; the launch traced here: 61.9 us
  Pallas kernels  57.7 us (93%)
  local copies, waits for them, and re-layouts  3.53 us (6%)
  between operations  0.65 us (1%)
    pallas_call x1, Pallas kernels, local(): pl.pallas_call(functools.partial(kernel, nseq, ngrp, nhead), out_shape=(j...  57.7 us
    unnamed x6, local copies, waits for them, and re-layouts  3.53 us

profile of v4, /device:TPU:4, one launch (start us, length us, event | category | flops | bytes accessed | tf_op | source)
XLA Modules:
  0.0 61.9 jit_solution(11668380159555070969)
XLA Ops:
  0.6 0.0 copy-start
  0.6 0.7 %copy-done = s32[4,2]{0,1:T(2,128)S(1)} copy-done((s32[4,2]{0,1:T(2,128)S(1)}, s32[4,2]{0,1:T(2,128)}, u32[]{:S(2)}) %copy-start) | copy-done | bytes 56
  1.3 57.7 %distill_backward.1 = (bf16[4,128,1024]{2,1,0:T(8,128)(2,1)S(1)}, bf16[4,128,128]{2,1,0:T(8,128)(2,1)S(1)}, bf16[4,128,128]{2,1,0:T(8,128)(2,1)S(1)}, f32[4,128]{1,0:T(4,128)S(1)}) custom-call(bf16[4,128,1024]{2,1,0:T(8,128)(2,1)} %bitcast.13, bf16[512,128]{1,0:T(8,128)(2,1)} %k_h.1, bf16[512,128]{1,0:T(8,128)(2,1)} %v_h.1, bf16[4,128,1024]{2,1,0:T(8,128)(2,1)} %bitcast.14, ...), custom_call_target="tpu_custom_call" | custom-call | tf_op jit(solution)/shard_map/distill_backward/pallas_call | solution.py:466
  59.0 1.0 %copy.16 = bf16[512,1024]{1,0:T(8,128)(2,1)} copy(bf16[512,1024]{1,0:T(8,128)(2,1)S(1)} %bitcast.8) | data formatting | bytes 2097152
  60.0 0.7 %copy.17 = bf16[512,128]{1,0:T(8,128)(2,1)} copy(bf16[512,128]{1,0:T(8,128)(2,1)S(1)} %bitcast.10) | data formatting | bytes 262144
  60.7 0.7 %copy.18 = bf16[512,128]{1,0:T(8,128)(2,1)} copy(bf16[512,128]{1,0:T(8,128)(2,1)S(1)} %bitcast.9) | data formatting | bytes 262144
  61.3 0.6 copy.19
Async XLA Ops:
  0.6 0.7 %copy-start = (s32[4,2]{0,1:T(2,128)S(1)}, s32[4,2]{0,1:T(2,128)}, u32[]{:S(2)}) copy-start(s32[4,2]{0,1:T(2,128)} %param.14) | copy-start | bytes 100
